TPU v7x, 32 devices: a whole 2x2x4 slice. The times are simulated.
32 devices in a mesh: groups: 2 (over x), band: 16 (over z, y, core).
Axes of the slice: x: 2, y: 2, z: 4, core: 2. Of those that a mesh axis runs over, the one named last changes fastest.
Arguments:
- queries: bfloat16 [128, 80, 2560], P(('groups', 'band')), parts along dimension 0, may hold values from -7 to 7, as said below
- kv_frames: bfloat16 [4, 4, 64, 80, 2560], P('groups', None, 'band'), parts along dimension 0, may hold values from -7 to 7
- frame_mask: int32 [6], P('groups'), parts along dimension 0, may hold values 0 or 1
- col_shift: int32 [128], P('groups'), parts along dimension 0, may hold values from -4 to 4
- latent: bfloat16 [6, 128, 2560], P('groups', 'band'), parts along dimension 0, may hold values from -6 to 6
- conv_in: bfloat16 [432, 384], replicated, may hold values from -0.3125 to 0.3125
- bias_in: float32 [384], replicated, may hold values from -3 to 3
- norm_gain: float32 [384], replicated, may hold values from 0.1 to 1.9
- conv_mid: bfloat16 [3456, 384], replicated, may hold values from -0.109375 to 0.109375
- bias_mid: float32 [384], replicated, may hold values from -3 to 3
Outputs:
- attended: bfloat16 [128, 80, 2560], P(('groups', 'band')), parts along dimension 0
- decoded: bfloat16 [256, 160, 384], P(('groups', 'band')), parts along dimension 0
There are 2 independent parts, one for each index of `groups`. A program takes and returns all parts, laid end to end along the dimension named above; an argument that names none is the same for every part. Nothing has to cross between parts.
Inputs may be any that keep to these rules, and one draw needn't show every extreme that they name: queries of a few patches may be large.
All inputs are finite; a program needn't handle non-finite values.
Results may differ from a plain program's by a relative error of at most 0.007.
Values may be sent and summed in bfloat16 or wider, within the bound.
A program may use at most 256 MiB of HBM per device.

v0:
```python
import math

import jax
import jax.numpy as jnp
from jax import lax
from jax.sharding import PartitionSpec as P

H = 20
HD = 128
RC = 8
SHIFT = 4


def padded_2(block, sides, width):
    for axis, dim in sides:
        count = lax.axis_size(axis)
        forward = [(i, i + 1) for i in range(count - 1)]
        backward = [(target, source) for source, target in forward]
        low = lax.ppermute(
            lax.slice_in_dim(block, block.shape[dim] - width, None, axis=dim), axis, forward
        )
        high = lax.ppermute(lax.slice_in_dim(block, 0, width, axis=dim), axis, backward)
        block = jnp.concatenate([low, block, high], axis=dim)
    return block


def entry_at(table, where_at):
    return lax.dynamic_index_in_dim(table, where_at, 0, keepdims=False)


def attend(query_row, window, row_ok, col_offset, frame_ok):
    width_c = query_row.shape[0]
    frames = window.shape[1]
    span = window.shape[2]
    reach = RC + SHIFT
    block = 16
    padded = jnp.pad(window, ((0, 0), (0, 0), (0, 0), (reach, reach), (0, 0)))
    padded = padded.reshape(2, frames, span, width_c + 2 * reach, H, HD)
    numerators = []
    maxima = []
    totals = []
    for start_col in range(0, width_c, block):
        keys_tile = padded[0, :, :, start_col : start_col + block + 2 * reach]
        values_tile = padded[1, :, :, start_col : start_col + block + 2 * reach]
        query_tile = query_row[start_col : start_col + block].reshape(block, H, HD)
        scores = jnp.einsum(
            "bhd,fnkhd->hbfnk", query_tile, keys_tile, preferred_element_type=jnp.float32
        ) * (1.0 / math.sqrt(HD))
        key_cols = start_col - reach + jnp.arange(block + 2 * reach, dtype=jnp.int32)
        query_cols = start_col + jnp.arange(block, dtype=jnp.int32)
        column_ok = (
            (key_cols[None, :] >= 0)
            & (key_cols[None, :] < width_c)
            & (jnp.abs(key_cols[None, :] - query_cols[:, None] - col_offset) <= RC)
        )
        valid = (
            column_ok[:, None, None, :]
            & frame_ok[None, :, None, None]
            & row_ok[None, None, :, None]
        )
        scores = jnp.where(valid[None], scores, -1e30)
        row_max = jnp.max(scores, axis=(2, 3, 4))
        weights = jnp.where(valid[None], jnp.exp(scores - row_max[:, :, None, None, None]), 0.0)
        row_sum = jnp.sum(weights, axis=(2, 3, 4))
        numerator = jnp.einsum(
            "hbfnk,fnkhd->bhd",
            weights.astype(jnp.bfloat16),
            values_tile,
            preferred_element_type=jnp.float32,
        )
        numerators.append(numerator)
        maxima.append(row_max)
        totals.append(row_sum)
    return (
        jnp.concatenate(numerators, axis=0),
        jnp.concatenate(maxima, axis=1),
        jnp.concatenate(totals, axis=1),
    )


def finish(numerator, row_sum):
    result = numerator / jnp.transpose(row_sum)[:, :, None]
    return result.reshape(numerator.shape[0], -1).astype(jnp.bfloat16)


def conv_first(source, out_rows, conv_in, bias_in):
    channels = conv_in.shape[0] // 27
    width_x = source.shape[2] // channels
    grid = source.reshape(3, source.shape[1], width_x, channels)
    grid = jnp.pad(grid, ((0, 0), (0, 0), (1, 1), (0, 0)))
    pieces = []
    for delta_t in range(3):
        for delta_y in range(3):
            for delta_x in range(3):
                pieces.append(
                    grid[delta_t, delta_y : delta_y + out_rows, delta_x : delta_x + width_x, :]
                )
    patches = jnp.concatenate(pieces, axis=-1).reshape(out_rows * width_x, 27 * channels)
    hidden = jnp.dot(patches, conv_in, preferred_element_type=jnp.float32) + bias_in
    return hidden.reshape(out_rows, width_x, conv_in.shape[1])


def activate(hidden, norm_gain):
    scale = lax.rsqrt(jnp.mean(hidden * hidden, axis=-1, keepdims=True) + 1e-06)
    return jax.nn.silu(hidden * scale * norm_gain)


def conv_second(active, out_rows, conv_mid):
    width_x = active.shape[1]
    grid = jnp.pad(active, ((0, 0), (1, 1), (0, 0)))
    pieces = []
    for delta_y in range(3):
        for delta_x in range(3):
            pieces.append(grid[delta_y : delta_y + out_rows, delta_x : delta_x + width_x, :])
    patches = jnp.concatenate(pieces, axis=-1).reshape(out_rows * width_x, conv_mid.shape[0])
    result = jnp.dot(patches, conv_mid, preferred_element_type=jnp.float32)
    return result.reshape(out_rows, width_x, conv_mid.shape[1])


def body(
    queries,
    kv_frames,
    frame_mask,
    col_shift,
    latent,
    conv_in,
    bias_in,
    norm_gain,
    conv_mid,
    bias_mid,
):
    band_count = lax.axis_size("band")
    band_place = lax.axis_index("band")
    rows_dev = queries.shape[0]
    total_rows = rows_dev * band_count
    first_row = band_place * rows_dev
    frame_ok = jnp.concatenate([frame_mask == 1, jnp.ones((1,), dtype=bool)])
    outputs = []
    padded = padded_2(kv_frames, (("band", 2),), 1)
    for row_at in range(rows_dev):
        global_row = first_row + row_at
        key_rows = global_row + jnp.arange(3, dtype=jnp.int32) - 1
        row_ok = (key_rows >= 0) & (key_rows < total_rows)
        numerator, row_max, row_sum = attend(
            queries[row_at],
            padded[:, :, row_at : row_at + 3],
            row_ok,
            entry_at(col_shift, global_row),
            frame_ok,
        )
        outputs.append(finish(numerator, row_sum))
    attended = jnp.stack(outputs)
    lat_rows = latent.shape[1]
    rim_width = 1
    lat_pad = padded_2(latent, (("band", 1),), rim_width)
    first = conv_first(lat_pad, lat_rows, conv_in, bias_in)
    active = padded_2(activate(first, norm_gain).astype(jnp.bfloat16), (("band", 0),), 1)
    decoded = (conv_second(active, lat_rows, conv_mid) + bias_mid + first).astype(jnp.bfloat16)
    return (attended, decoded)


def solution(mesh):
    placed = (
        P(("groups", "band"), None, None),
        P("groups", None, "band", None, None),
        P("groups"),
        P("groups"),
        P("groups", "band", None),
        P(),
        P(),
        P(),
        P(),
        P(),
    )
    return jax.shard_map(
        body,
        mesh=mesh,
        in_specs=placed,
        out_specs=(P(("groups", "band"), None, None), P(("groups", "band"), None, None)),
        check_vma=False,
    )
```

profile of v0, /device:TPU:21, one launch (start us, length us, event | category | flops | bytes accessed | tf_op | source)
XLA Modules:
  0.0 524.1 jit_solution(8990256302153897304)
XLA Ops:
  0.6 1.8 fusion.237
  2.4 3.7 collective-permute-start.2
  6.1 1.9 collective-permute-start.3
  8.1 6.4 %fusion.232 = (bf16[2,4,1,80,2560]{4,3,2,1,0:T(8,128)(2,1)}, bf16[2,4,1,80,2560]{4,3,2,1,0:T(8,128)(2,1)}) fusion(bf16[2,4,4,80,2560]{4,3,2,1,0:T(8,128)(2,1)} %param.11), kind=kLoop, calls=%fused_computation.454 | loop fusion | bytes 13107200 | tf_op jit(solution)/shard_map/slice | solution.py:20
  14.4 4.5 collective-permute-start
  19.0 1.9 collective-permute-start.1
  30.4 15.4 %fusion.233 = (bf16[2,4,3,80,2560]{4,3,2,1,0:T(8,128)(2,1)}, bf16[2,4,3,80,2560]{4,3,2,1,0:T(8,128)(2,1)}) fusion(bf16[2,4,4,80,2560]{4,3,2,1,0:T(8,128)(2,1)} %param.11), kind=kLoop, calls=%fused_computation.455 | loop fusion | bytes 39321600 | tf_op jit(solution)/shard_map/slice | solution.py:146
  46.3 2.3 fusion.234
  53.8 10.1 %pad.22 = bf16[2,4,3,104,2560]{4,3,2,1,0:T(8,128)(2,1)} pad(bf16[2,4,3,80,2560]{4,3,2,1,0:T(8,128)(2,1)} %get-tuple-element.46, bf16[]{:T(256)} %constant.29.clone.1), padding=0_0x0_0x0_0x12_12x0_0 | pad | bytes 22609922 | tf_op jit(solution)/shard_map/jit(_pad)/pad | solution.py:37
  64.0 21.9 %reshape.1520 = bf16[2,4,3,104,20,128]{5,4,3,2,1,0:T(8,128)(2,1)} reshape(bf16[2,4,3,104,2560]{4,3,2,1,0:T(8,128)(2,1)} %pad.22) | data formatting | bytes 25559040 | tf_op jit(solution)/shard_map/reshape | solution.py:38
  85.9 10.1 %pad.23 = bf16[2,4,3,104,2560]{4,3,2,1,0:T(8,128)(2,1)} pad(bf16[2,4,3,80,2560]{4,3,2,1,0:T(8,128)(2,1)} %get-tuple-element.47, bf16[]{:T(256)} %constant.29.clone.1), padding=0_0x0_0x0_0x12_12x0_0 | pad | bytes 22609922 | tf_op jit(solution)/shard_map/jit(_pad)/pad | solution.py:37
  96.0 21.9 %reshape.1526 = bf16[2,4,3,104,20,128]{5,4,3,2,1,0:T(8,128)(2,1)} reshape(bf16[2,4,3,104,2560]{4,3,2,1,0:T(8,128)(2,1)} %pad.23) | data formatting | bytes 25559040 | tf_op jit(solution)/shard_map/reshape | solution.py:38
  118.1 22.3 %fusion.230 = (bf16[1,4,3,40,20,128]{5,4,3,2,1,0:T(8,128)(2,1)}, bf16[1,4,3,40,20,128]{5,4,3,2,1,0:T(8,128)(2,1)}, bf16[1,4,3,40,20,128]{5,4,3,2,1,0:T(8,128)(2,...) fusion(bf16[2,4,3,104,20,128]{5,4,3,2,1,0:T(8,128)(2,1)} %resha, ...), kind=kLoop, calls=%fused_computation.452 | loop fusion | bytes 49152000 | tf_op jit(solution)/shard_map/slice | solution.py:43
  141.2 2.6 fusion.227
  143.9 3.2 fusion.208
  147.1 2.7 fusion.219
  150.7 4.7 fusion.61
  158.7 4.7 fusion.60
  166.7 4.7 fusion.59
  174.8 5.2 fusion.58
  183.3 4.7 fusion.57
  188.0 1.7 fusion.92
  189.8 2.8 fusion.124
  196.0 20.6 %fusion.229 = (bf16[1,4,3,40,20,128]{5,4,3,2,1,0:T(8,128)(2,1)S(1)}, bf16[1,4,3,40,20,128]{5,4,3,2,1,0:T(8,128)(2,1)}, bf16[1,4,3,40,20,128]{5,4,3,2,1,0:T(8,128...) fusion(bf16[2,4,3,104,20,128]{5,4,3,2,1,0:T(8,128)(2,1)} %resha, ...), kind=kLoop, calls=%fused_computation.451 | loop fusion | bytes 49152000 | tf_op jit(solution)/shard_map/slice | solution.py:43
  217.5 2.9 fusion.56
  224.8 4.8 fusion.55
  234.5 4.8 fusion.54
  244.2 5.0 fusion.53
  254.0 4.8 fusion.52
  258.8 2.2 fusion.82
  263.9 2.8 fusion.119
  270.6 2.0 div.85
  272.7 2.2 div.86
  279.6 1.7 constant_dynamic-update-slice_fusion.11
  282.9 2.0 divide_convert_fusion.1
  295.9 1.9 reshape.1538
  297.8 2.7 fusion.235
  300.5 2.0 pad_slice_fusion
  302.4 2.1 pad_slice_fusion.1
  304.5 9.0 %concatenate.238 = bf16[1280,432]{1,0:T(8,128)(2,1)} concatenate(bf16[1280,16]{1,0:T(8,128)(2,1)} %bitcast.604, bf16[1280,16]{1,0:T(8,128)(2,1)} %bitcast.603, bf16[1280,16]{1,0:T(8,128)(2,1)} %bitcast.606, bf16[1280,16]{1,0:T(8,128)(2,1)} %bitcast.607, bf16[1280,16]{1,0:T(8,128)(2,1)} %bitcast.602, bf16[1280,16]{1,0:T(8,128)(2,1)} %bitcast.608, bf16[1280,16]{1,0:T(8,128)(2,1)} %bitcast.609, ...), dimensions={1} | concatenate | bytes 2211840 | tf_op jit(solution)/shard_map/concatenate | solution.py:98
  313.5 3.5 multiply_reduce_fusion
  317.1 2.1 multiply_convert_fusion
  319.3 4.5 collective-permute-start.4
  323.8 1.9 collective-permute-start.5
  326.0 5.0 collective-permute-done.5
  335.1 5.9 %add_convert_fusion = bf16[8,160,384]{2,1,0:T(8,128)(2,1)} fusion(f32[8,160,384]{2,1,0:T(8,128)S(1)} %bitcast.598, bf16[8,160,3456]{2,1,0:T(8,128)(2,1)S(1)} %slice_dynamic-update-slice_fusion, bf16[3456,384]{1,0:T(8,128)(2,1)S(1)} %copy-done, f32[384]{0:T(512)S(1)} %copy-done.91), kind=kOutput, calls=%fused_computation.113 | convolution fusion | flops 3398860800 | bytes 14452224 | tf_op jit(solution)/shard_map/dot_general | solution.py:116
  341.0 12.9 %fusion.3 = (bf16[2,4,3,104,2560]{4,3,2,1,0:T(8,128)(2,1)}, bf16[2,4,3,104,2560]{4,3,2,1,0:T(8,128)(2,1)}) fusion(bf16[2,4,4,80,2560]{4,3,2,1,0:T(8,128)(2,1)S(1)} %bitcast.595, bf16[2,4,1,80,2560]{4,3,2,1,0:T(8,128)(2,1)} %collective-permute-done, bf16[2,4,1,80,2560]{4,3,2,1,0:T(8,128)(2,1)} %collective-permute-done.1), kind=kLoop, calls=%fused_computation.6 | loop fusion | flops 95846400 | bytes 45219840 | tf_op jit(solution)/shard_map/concatenate | solution.py:23
  354.0 21.9 %reshape.1514 = bf16[2,4,3,104,20,128]{5,4,3,2,1,0:T(8,128)(2,1)} reshape(bf16[2,4,3,104,2560]{4,3,2,1,0:T(8,128)(2,1)} %get-tuple-element.42) | data formatting | bytes 25559040 | tf_op jit(solution)/shard_map/reshape | solution.py:38
  375.9 20.7 %fusion.228 = (bf16[1,4,3,40,20,128]{5,4,3,2,1,0:T(8,128)(2,1)S(1)}, bf16[1,4,3,40,20,128]{5,4,3,2,1,0:T(8,128)(2,1)}, bf16[1,4,3,40,20,128]{5,4,3,2,1,0:T(8,128...) fusion(bf16[2,4,3,104,20,128]{5,4,3,2,1,0:T(8,128)(2,1)} %resha, ...), kind=kLoop, calls=%fused_computation.450 | loop fusion | bytes 49152000 | tf_op jit(solution)/shard_map/slice | solution.py:43
  396.6 2.9 fusion.51
  401.7 4.7 fusion.50
  409.7 4.7 fusion.49
  417.7 4.9 fusion.48
  426.0 4.7 fusion.47
  430.7 1.7 fusion.72
  432.5 2.8 fusion.114
  435.8 21.9 %reshape.1532 = bf16[2,4,3,104,20,128]{5,4,3,2,1,0:T(8,128)(2,1)} reshape(bf16[2,4,3,104,2560]{4,3,2,1,0:T(8,128)(2,1)} %get-tuple-element.43) | data formatting | bytes 25559040 | tf_op jit(solution)/shard_map/reshape | solution.py:38
  457.8 20.9 %fusion.231 = (bf16[1,4,3,40,20,128]{5,4,3,2,1,0:T(8,128)(2,1)S(1)}, bf16[1,4,3,40,20,128]{5,4,3,2,1,0:T(8,128)(2,1)}, bf16[1,4,3,40,20,128]{5,4,3,2,1,0:T(8,128...) fusion(bf16[2,4,3,104,20,128]{5,4,3,2,1,0:T(8,128)(2,1)} %resha, ...), kind=kLoop, calls=%fused_computation.453 | loop fusion | bytes 49152000 | tf_op jit(solution)/shard_map/slice | solution.py:43
  478.7 2.9 fusion.66
  483.8 4.7 fusion.65
  491.8 4.7 fusion.64
  499.8 4.9 fusion.63
  508.0 4.7 fusion.62
  513.6 2.5 fusion.129
  (375 shorter events, 115.3 us)
Async XLA Ops:
  0.6 334.3 %copy-start = (bf16[3456,384]{1,0:T(8,128)(2,1)S(1)}, bf16[3456,384]{1,0:T(8,128)(2,1)}, u32[]{:S(2)}) copy-start(bf16[3456,384]{1,0:T(8,128)(2,1)} %param.18) | copy-start | bytes 7962628
  2.4 292.3 %collective-permute-start.2 = (bf16[3,1,2560]{2,1,0:T(2,128)(2,1)}, bf16[3,1,2560]{2,1,0:T(2,128)(2,1)}, u32[]{:S(2)}, u32[]{:S(2)}) collective-permute-start(bf16[3,1,2560]{2,1,0:T(2,128)(2,1)} %get-tuple-element.136), channel_id=1, source_target_pairs={{0,1},{1,2},{2,3},{3,4},{4,5},{5,6},{6,7},{7,8},{8,9},{9,10},{10,1... | collective-permute-start | bytes 46088 | tf_op jit(solution)/shard_map/ppermute | solution.py:19
  6.1 288.6 %collective-permute-start.3 = (bf16[3,1,2560]{2,1,0:T(2,128)(2,1)}, bf16[3,1,2560]{2,1,0:T(2,128)(2,1)}, u32[]{:S(2)}, u32[]{:S(2)}) collective-permute-start(bf16[3,1,2560]{2,1,0:T(2,128)(2,1)} %get-tuple-element.137), channel_id=1, source_target_pairs={{1,0},{2,1},{3,2},{4,3},{5,4},{6,5},{7,6},{8,7},{9,8},{10,9},{11,1... | collective-permute-start | bytes 46088 | tf_op jit(solution)/shard_map/ppermute | solution.py:22
  14.4 326.6 %collective-permute-start = (bf16[2,4,1,80,2560]{4,3,2,1,0:T(8,128)(2,1)}, bf16[2,4,1,80,2560]{4,3,2,1,0:T(8,128)(2,1)}, u32[]{:S(2)}, u32[]{:S(2)}) collective-permute-start(bf16[2,4,1,80,2560]{4,3,2,1,0:T(8,128)(2,1)} %get-tuple-element.44), channel_id=1, source_target_pairs={{0,1},{1,2},{2,3},{3,4},{4,5},{5,6},{6,7},{7,8},{8,9},{9,10},{10,1... | collective-permute-start | bytes 9830408 | tf_op jit(solution)/shard_map/ppermute | solution.py:19
  19.0 322.0 %collective-permute-start.1 = (bf16[2,4,1,80,2560]{4,3,2,1,0:T(8,128)(2,1)}, bf16[2,4,1,80,2560]{4,3,2,1,0:T(8,128)(2,1)}, u32[]{:S(2)}, u32[]{:S(2)}) collective-permute-start(bf16[2,4,1,80,2560]{4,3,2,1,0:T(8,128)(2,1)} %get-tuple-element.45), channel_id=1, source_target_pairs={{1,0},{2,1},{3,2},{4,3},{5,4},{6,5},{7,6},{8,7},{9,8},{10,9},{11,1... | collective-permute-start | bytes 9830408 | tf_op jit(solution)/shard_map/ppermute | solution.py:22
  30.4 15.4 %copy-start.92 = (s32[3]{0:T(128)S(1)}, s32[3]{0:T(128)}, u32[]{:S(2)}) copy-start(s32[3]{0:T(128)} %param.12) | copy-start | bytes 40
  117.9 22.4 %copy-start.93 = (pred[3]{0:T(512)(128)(4,1)S(1)}, pred[3]{0:T(512)(128)(4,1)}, u32[]{:S(2)}) copy-start(pred[3]{0:T(512)(128)(4,1)} %broadcast_compare_fusion) | copy-start | bytes 13
  117.9 22.5 %copy-start.71 = (s32[64]{0:T(128)S(1)}, s32[64]{0:T(128)}, u32[]{:S(2)}) copy-start(s32[64]{0:T(128)} %param.13) | copy-start | bytes 772
  117.9 23.2 %copy-start.82 = (s32[40]{0:T(128)S(1)}, s32[40]{0:T(128)}, u32[]{:S(2)}) copy-start(s32[40]{0:T(128)} %iota_add_fusion.7) | copy-start | bytes 484
  117.9 23.2 %copy-start.83 = (s32[16]{0:T(128)S(1)}, s32[16]{0:T(128)}, u32[]{:S(2)}) copy-start(s32[16]{0:T(128)} %iota_add_fusion.6) | copy-start | bytes 196
  117.9 23.2 %copy-start.84 = (pred[40]{0:T(512)(128)(4,1)S(1)}, pred[40]{0:T(512)(128)(4,1)}, u32[]{:S(2)}) copy-start(pred[40]{0:T(512)(128)(4,1)} %compare_and_fusion.6) | copy-start | bytes 124
  118.0 25.9 %copy-start.85 = (s32[40]{0:T(128)S(1)}, s32[40]{0:T(128)}, u32[]{:S(2)}) copy-start(s32[40]{0:T(128)} %iota_add_fusion.8) | copy-start | bytes 484
  118.0 25.9 %copy-start.86 = (s32[40]{0:T(128)S(1)}, s32[40]{0:T(128)}, u32[]{:S(2)}) copy-start(s32[40]{0:T(128)} %iota_add_fusion.1) | copy-start | bytes 484
  118.0 25.9 %copy-start.87 = (s32[16]{0:T(128)S(1)}, s32[16]{0:T(128)}, u32[]{:S(2)}) copy-start(s32[16]{0:T(128)} %iota_add_fusion) | copy-start | bytes 196
  118.0 25.9 %copy-start.88 = (pred[40]{0:T(512)(128)(4,1)S(1)}, pred[40]{0:T(512)(128)(4,1)}, u32[]{:S(2)}) copy-start(pred[40]{0:T(512)(128)(4,1)} %compare_and_fusion.8) | copy-start | bytes 124
  118.0 25.9 %copy-start.89 = (pred[40]{0:T(512)(128)(4,1)S(1)}, pred[40]{0:T(512)(128)(4,1)}, u32[]{:S(2)}) copy-start(pred[40]{0:T(512)(128)(4,1)} %compare_and_fusion.3) | copy-start | bytes 124
  118.0 29.1 %copy-start.76 = (s32[40]{0:T(128)S(1)}, s32[40]{0:T(128)}, u32[]{:S(2)}) copy-start(s32[40]{0:T(128)} %iota_add_fusion.5) | copy-start | bytes 484
  118.0 29.1 %copy-start.77 = (s32[16]{0:T(128)S(1)}, s32[16]{0:T(128)}, u32[]{:S(2)}) copy-start(s32[16]{0:T(128)} %iota_add_fusion.4) | copy-start | bytes 196
  118.0 29.1 %copy-start.78 = (s32[40]{0:T(128)S(1)}, s32[40]{0:T(128)}, u32[]{:S(2)}) copy-start(s32[40]{0:T(128)} %iota_add_fusion.3) | copy-start | bytes 484
  118.0 29.1 %copy-start.79 = (s32[16]{0:T(128)S(1)}, s32[16]{0:T(128)}, u32[]{:S(2)}) copy-start(s32[16]{0:T(128)} %iota_add_fusion.2) | copy-start | bytes 196
  118.0 29.1 %copy-start.80 = (pred[40]{0:T(512)(128)(4,1)S(1)}, pred[40]{0:T(512)(128)(4,1)}, u32[]{:S(2)}) copy-start(pred[40]{0:T(512)(128)(4,1)} %compare_and_fusion.5) | copy-start | bytes 124
  118.1 29.1 %copy-start.81 = (pred[40]{0:T(512)(128)(4,1)S(1)}, pred[40]{0:T(512)(128)(4,1)}, u32[]{:S(2)}) copy-start(pred[40]{0:T(512)(128)(4,1)} %compare_and_fusion.4) | copy-start | bytes 124
  118.1 32.5 %copy-start.75 = (pred[3]{0:T(512)(128)(4,1)S(1)}, pred[3]{0:T(512)(128)(4,1)}, u32[]{:S(2)}) copy-start(pred[3]{0:T(512)(128)(4,1)} %compare_and_fusion.1) | copy-start | bytes 13
  118.1 32.6 %copy-start.55 = (bf16[16,20,128]{2,1,0:T(8,128)(2,1)S(1)}, bf16[16,20,128]{2,1,0:T(8,128)(2,1)}, u32[]{:S(2)}) copy-start(bf16[16,20,128]{2,1,0:T(8,128)(2,1)} %reshape.1531) | copy-start | bytes 245764
  140.5 15.0 %copy-start.72 = (pred[4]{0:T(512)(128)(4,1)}, pred[4]{0:T(512)(128)(4,1)S(1)}, u32[]{:S(2)}) copy-start(pred[4]{0:T(512)(128)(4,1)S(1)} %pad_add_fusion) | copy-start | bytes 16
  196.0 20.7 %copy-start.64 = (pred[16,4,40]{2,0,1:T(8,128)(4,1)S(1)}, pred[16,4,40]{2,0,1:T(8,128)(4,1)}, u32[]{:S(2)}) copy-start(pred[16,4,40]{2,0,1:T(8,128)(4,1)} %get-tuple-element.167) | copy-start | bytes 7684
  196.0 20.7 %copy-start.65 = (pred[16,4,40]{2,0,1:T(8,128)(4,1)S(1)}, pred[16,4,40]{2,0,1:T(8,128)(4,1)}, u32[]{:S(2)}) copy-start(pred[16,4,40]{2,0,1:T(8,128)(4,1)} %get-tuple-element.168) | copy-start | bytes 7684
  196.0 20.7 %copy-start.66 = (pred[16,4,40]{2,0,1:T(8,128)(4,1)S(1)}, pred[16,4,40]{2,0,1:T(8,128)(4,1)}, u32[]{:S(2)}) copy-start(pred[16,4,40]{2,0,1:T(8,128)(4,1)} %get-tuple-element.169) | copy-start | bytes 7684
  196.0 20.7 %copy-start.67 = (pred[16,4,40]{2,0,1:T(8,128)(4,1)S(1)}, pred[16,4,40]{2,0,1:T(8,128)(4,1)}, u32[]{:S(2)}) copy-start(pred[16,4,40]{2,0,1:T(8,128)(4,1)} %get-tuple-element.170) | copy-start | bytes 7684
  196.0 20.7 %copy-start.68 = (pred[16,4,40]{2,0,1:T(8,128)(4,1)S(1)}, pred[16,4,40]{2,0,1:T(8,128)(4,1)}, u32[]{:S(2)}) copy-start(pred[16,4,40]{2,0,1:T(8,128)(4,1)} %get-tuple-element.171) | copy-start | bytes 7684
  196.0 20.7 %copy-start.74 = (pred[3]{0:T(512)(128)(4,1)S(1)}, pred[3]{0:T(512)(128)(4,1)}, u32[]{:S(2)}) copy-start(pred[3]{0:T(512)(128)(4,1)} %compare_and_fusion.2) | copy-start | bytes 13
  196.0 21.5 %copy-start.49 = (bf16[16,20,128]{2,1,0:T(8,128)(2,1)S(1)}, bf16[16,20,128]{2,1,0:T(8,128)(2,1)}, u32[]{:S(2)}) copy-start(bf16[16,20,128]{2,1,0:T(8,128)(2,1)} %reshape.1525) | copy-start | bytes 245764
  224.8 4.8 copy-start.43
  234.5 4.8 copy-start.42
  244.2 5.0 copy-start.41
  254.0 4.8 copy-start.40
  274.9 10.0 %copy-start.20 = (f32[1,80,2560]{2,1,0:T(8,128)S(1)}, f32[1,80,2560]{2,1,0:T(8,128)}, u32[]{:S(2)}) copy-start(f32[1,80,2560]{2,1,0:T(8,128)} %constant_dynamic-update-slice_fusion.9) | copy-start | bytes 2457604
  274.9 10.0 %copy-start.28 = (f32[1,16,2560]{2,1,0:T(8,128)S(1)}, f32[1,16,2560]{2,1,0:T(8,128)}, u32[]{:S(2)}) copy-start(f32[1,16,2560]{2,1,0:T(8,128)} %concatenate.189) | copy-start | bytes 491524
  274.9 10.1 %copy-start.26 = (f32[1,16,2560]{2,1,0:T(8,128)S(1)}, f32[1,16,2560]{2,1,0:T(8,128)}, u32[]{:S(2)}) copy-start(f32[1,16,2560]{2,1,0:T(8,128)} %concatenate.190) | copy-start | bytes 491524
  276.3 8.7 %copy-start.24 = (f32[1,16,2560]{2,1,0:T(8,128)S(1)}, f32[1,16,2560]{2,1,0:T(8,128)}, u32[]{:S(2)}) copy-start(f32[1,16,2560]{2,1,0:T(8,128)} %concatenate.191) | copy-start | bytes 491524
  278.0 7.1 %copy-start.22 = (f32[1,16,2560]{2,1,0:T(8,128)S(1)}, f32[1,16,2560]{2,1,0:T(8,128)}, u32[]{:S(2)}) copy-start(f32[1,16,2560]{2,1,0:T(8,128)} %concatenate.192) | copy-start | bytes 491524
  279.6 5.5 %copy-start.4 = (f32[1,80,2560]{2,1,0:T(8,128)S(1)}, f32[1,80,2560]{2,1,0:T(8,128)}, u32[]{:S(2)}) copy-start(f32[1,80,2560]{2,1,0:T(8,128)} %div.86) | copy-start | bytes 2457604
  284.9 4.1 copy-start.36
  285.0 4.8 copy-start.35
  285.0 5.5 %copy-start.34 = (bf16[1,16,2560]{2,1,0:T(8,128)(2,1)S(1)}, bf16[1,16,2560]{2,1,0:T(8,128)(2,1)}, u32[]{:S(2)}) copy-start(bf16[1,16,2560]{2,1,0:T(8,128)(2,1)} %get-tuple-element.91) | copy-start | bytes 245764
  285.0 6.2 %copy-start.33 = (bf16[1,16,2560]{2,1,0:T(8,128)(2,1)S(1)}, bf16[1,16,2560]{2,1,0:T(8,128)(2,1)}, u32[]{:S(2)}) copy-start(bf16[1,16,2560]{2,1,0:T(8,128)(2,1)} %get-tuple-element.102) | copy-start | bytes 245764
  285.1 6.8 %copy-start.32 = (bf16[1,16,2560]{2,1,0:T(8,128)(2,1)S(1)}, bf16[1,16,2560]{2,1,0:T(8,128)(2,1)}, u32[]{:S(2)}) copy-start(bf16[1,16,2560]{2,1,0:T(8,128)(2,1)} %get-tuple-element.103) | copy-start | bytes 245764
  285.1 7.5 %copy-start.31 = (bf16[1,16,2560]{2,1,0:T(8,128)(2,1)S(1)}, bf16[1,16,2560]{2,1,0:T(8,128)(2,1)}, u32[]{:S(2)}) copy-start(bf16[1,16,2560]{2,1,0:T(8,128)(2,1)} %get-tuple-element.104) | copy-start | bytes 245764
  285.1 8.2 %copy-start.30 = (bf16[1,16,2560]{2,1,0:T(8,128)(2,1)S(1)}, bf16[1,16,2560]{2,1,0:T(8,128)(2,1)}, u32[]{:S(2)}) copy-start(bf16[1,16,2560]{2,1,0:T(8,128)(2,1)} %get-tuple-element.105) | copy-start | bytes 245764
  304.5 9.0 %copy-start.90 = (f32[384]{0:T(512)S(1)}, f32[384]{0:T(512)}, u32[]{:S(2)}) copy-start(f32[384]{0:T(512)} %param.16) | copy-start | bytes 4612
  317.0 8.8 %copy-start.56 = (pred[16,4,40]{2,0,1:T(8,128)(4,1)S(1)}, pred[16,4,40]{2,0,1:T(8,128)(4,1)}, u32[]{:S(2)}) copy-start(pred[16,4,40]{2,0,1:T(8,128)(4,1)} %get-tuple-element.177) | copy-start | bytes 7684
  317.0 8.8 %copy-start.57 = (pred[16,4,40]{2,0,1:T(8,128)(4,1)S(1)}, pred[16,4,40]{2,0,1:T(8,128)(4,1)}, u32[]{:S(2)}) copy-start(pred[16,4,40]{2,0,1:T(8,128)(4,1)} %get-tuple-element.178) | copy-start | bytes 7684
  317.0 8.8 %copy-start.58 = (pred[16,4,40]{2,0,1:T(8,128)(4,1)S(1)}, pred[16,4,40]{2,0,1:T(8,128)(4,1)}, u32[]{:S(2)}) copy-start(pred[16,4,40]{2,0,1:T(8,128)(4,1)} %get-tuple-element.179) | copy-start | bytes 7684
  317.0 8.8 %copy-start.59 = (pred[16,4,40]{2,0,1:T(8,128)(4,1)S(1)}, pred[16,4,40]{2,0,1:T(8,128)(4,1)}, u32[]{:S(2)}) copy-start(pred[16,4,40]{2,0,1:T(8,128)(4,1)} %get-tuple-element.180) | copy-start | bytes 7684
  317.0 8.8 %copy-start.69 = (pred[16,4,40]{2,0,1:T(8,128)(4,1)S(1)}, pred[16,4,40]{2,0,1:T(8,128)(4,1)}, u32[]{:S(2)}) copy-start(pred[16,4,40]{2,0,1:T(8,128)(4,1)} %get-tuple-element.182) | copy-start | bytes 7684
  319.3 6.7 %collective-permute-start.4 = (bf16[1,160,384]{2,1,0:T(8,128)(2,1)S(1)}, bf16[1,160,384]{2,1,0:T(8,128)(2,1)S(1)}, u32[]{:S(2)}, u32[]{:S(2)}) collective-permute-start(bf16[1,160,384]{2,1,0:T(8,128)(2,1)S(1)} %get-tuple-element.134), channel_id=1, source_target_pairs={{0,1},{1,2},{2,3},{3,4},{4,5},{5,6},{6,7},{7,8},{8,9},{9,10},{10,1... | collective-permute-start | bytes 368648 | tf_op jit(solution)/shard_map/ppermute | solution.py:19
  323.8 7.1 %collective-permute-start.5 = (bf16[1,160,384]{2,1,0:T(8,128)(2,1)S(1)}, bf16[1,160,384]{2,1,0:T(8,128)(2,1)S(1)}, u32[]{:S(2)}, u32[]{:S(2)}) collective-permute-start(bf16[1,160,384]{2,1,0:T(8,128)(2,1)S(1)} %get-tuple-element.135), channel_id=1, source_target_pairs={{1,0},{2,1},{3,2},{4,3},{5,4},{6,5},{7,6},{8,7},{9,8},{10,9},{11,1... | collective-permute-start | bytes 368648 | tf_op jit(solution)/shard_map/ppermute | solution.py:22
  334.6 6.4 %slice-start = ((s8[13107200]{0:T(1024)(128)(4,1)}), s8[4194304]{0:T(1024)(128)(4,1)S(1)}, s32[]{:S(2)}) async-start(s8[13107200]{0:T(1024)(128)(4,1)} %bitcast.594), calls=%async_computation | async-start | bytes 8388608
  335.1 5.9 %slice-start.1 = ((s8[13107200]{0:T(1024)(128)(4,1)}), s8[4194304]{0:T(1024)(128)(4,1)S(1)}, s32[]{:S(2)}) async-start(s8[13107200]{0:T(1024)(128)(4,1)} %bitcast.594), calls=%async_computation.1 | async-start | bytes 8388608
  335.1 5.9 %slice-start.2 = ((s8[13107200]{0:T(1024)(128)(4,1)}), s8[4194304]{0:T(1024)(128)(4,1)S(1)}, s32[]{:S(2)}) async-start(s8[13107200]{0:T(1024)(128)(4,1)} %bitcast.594), calls=%async_computation.2 | async-start | bytes 8388608
  335.1 5.9 %slice-start.3 = ((s8[13107200]{0:T(1024)(128)(4,1)}), s8[524288]{0:T(1024)(128)(4,1)S(1)}, s32[]{:S(2)}) async-start(s8[13107200]{0:T(1024)(128)(4,1)} %bitcast.594), calls=%async_computation.3 | async-start | bytes 1048576
  375.9 20.7 %copy-start.39 = (pred[16,4,3,40]{3,0,2,1:T(8,128)(4,1)S(1)}, pred[16,4,3,40]{3,0,2,1:T(8,128)(4,1)}, u32[]{:S(2)}) copy-start(pred[16,4,3,40]{3,0,2,1:T(8,128)(4,1)} %get-tuple-element.158) | copy-start | bytes 23044
  375.9 20.7 %copy-start.54 = (bf16[16,20,128]{2,1,0:T(8,128)(2,1)S(1)}, bf16[16,20,128]{2,1,0:T(8,128)(2,1)}, u32[]{:S(2)}) copy-start(bf16[16,20,128]{2,1,0:T(8,128)(2,1)} %reshape.1519) | copy-start | bytes 245764
  457.8 20.9 %copy-start.48 = (bf16[16,20,128]{2,1,0:T(8,128)(2,1)S(1)}, bf16[16,20,128]{2,1,0:T(8,128)(2,1)}, u32[]{:S(2)}) copy-start(bf16[16,20,128]{2,1,0:T(8,128)(2,1)} %reshape.1537) | copy-start | bytes 245764
  (40 other events, 78.5 us)
where the time goes:
time: 534 us; the launch traced here: 524 us
  local copies, waits for them, and re-layouts  312 us (58%)
  matrix products  121 us (23%)
  other arithmetic  65.6 us (12%)
  starting transfers between devices  18.5 us (3%)
    dot_general x20, matrix products, attend(): jnp.einsum('bhd,fnkhd->hbfnk', query_tile, keys_tile, preferred_element_t...  90 us
    reshape x4, local copies, waits for them, and re-layouts, attend(): padded = padded.reshape(2, frames, span, width_c + 2 * reach, H, HD)  87.6 us
    slice x4, local copies, waits for them, and re-layouts, attend(): keys_tile = padded[0, :, :, start_col:start_col + block + 2 * reach]  84.5 us
    unnamed x217, local copies, waits for them, and re-layouts  26.6 us
    dot_general x20, matrix products, attend(): jnp.einsum('hbfnk,fnkhd->bhd', weights.astype(jnp.bfloat16), values_tile,...  21.9 us
    reduce_sum x20, other arithmetic, attend(): row_sum = jnp.sum(weights, axis=(2, 3, 4))  20.9 us
    pad x2, local copies, waits for them, and re-layouts, attend(): padded = jnp.pad(window, ((0, 0), (0, 0), (0, 0), (reach, reach), (0, 0)))  20.3 us
    concatenate x24, local copies, waits for them, and re-layouts, attend(): jnp.concatenate(numerators, axis=0)  19.1 us
  transfers between devices with their start and end apart: 6, of which 1 were waited for; matrix products, arithmetic and copies ran while one was open for 59% of the time, Pallas kernels for 0%

commit v1 on v0

v1 whole, which is shorter than its diff:
```python
import functools
import math

import jax
import jax.numpy as jnp
from jax import lax
from jax.experimental import pallas as pl
from jax.experimental.pallas import tpu as pltpu
from jax.sharding import PartitionSpec as P

HD = 128
RC = 8
NEG = -1e30
SCALE = 1.0 / math.sqrt(HD)
HEADS_PER_STEP = 2


def to_next(block, axis):
    count = lax.axis_size(axis)
    return lax.ppermute(block, axis, [(i, i + 1) for i in range(count - 1)])


def to_previous(block, axis):
    count = lax.axis_size(axis)
    return lax.ppermute(block, axis, [(i + 1, i) for i in range(count - 1)])


def window_bias(key_cols, frame_bias, offset, cols):
    width = key_cols.shape[1]
    query_cols = lax.broadcasted_iota(jnp.int32, (cols, width), 0)
    ok = jnp.abs(key_cols - query_cols - offset) <= RC
    return jnp.where(ok, frame_bias, NEG)


def partial_attention(query, keys, values, bias):
    scores = lax.dot_general(
        query, keys, (((1,), (1,)), ((), ())), preferred_element_type=jnp.float32
    )
    scores = scores + bias
    top = jnp.max(scores, axis=-1, keepdims=True)
    weights = jnp.exp((scores - top) * SCALE)
    total = jnp.sum(weights, axis=-1, keepdims=True)
    numerator = jnp.dot(weights.astype(jnp.bfloat16), values, preferred_element_type=jnp.float32)
    return numerator * (1.0 / total), top * SCALE + jnp.log(total)


def edge_kernel(
    offsets, cols_ref, fb_ref, qp_ref, qn_ref, kvf_ref, kvl_ref, op_ref, on_ref, lp_ref, ln_ref, bias_ref
):
    step = pl.program_id(0)
    frames, cols = kvf_ref.shape[1], qp_ref.shape[1]

    @pl.when(step == 0)
    def _():
        for side in range(2):
            bias_ref[side] = window_bias(cols_ref[...], fb_ref[...], offsets[side], cols)
        lp_ref[...] = jnp.zeros_like(lp_ref)
        ln_ref[...] = jnp.zeros_like(ln_ref)

    lane = lax.broadcasted_iota(jnp.int32, lp_ref.shape, 1)
    for j in range(HEADS_PER_STEP):
        part = pl.ds(j * HD, HD)
        sides = ((qp_ref, kvf_ref, op_ref, lp_ref), (qn_ref, kvl_ref, on_ref, ln_ref))
        for side, (q_ref, kv_ref, o_ref, l_ref) in enumerate(sides):
            keys = jnp.concatenate([kv_ref[0, f, 0, :, part] for f in range(frames)], axis=0)
            values = jnp.concatenate([kv_ref[1, f, 0, :, part] for f in range(frames)], axis=0)
            out, level = partial_attention(q_ref[0, :, part], keys, values, bias_ref[side])
            o_ref[0, :, part] = out.astype(jnp.bfloat16)
            l_ref[...] = jnp.where(lane == step * HEADS_PER_STEP + j, level, l_ref[...])


def main_kernel(
    offsets, cols_ref, fb_ref, q_ref, kv_ref, op_ref, on_ref, lp_ref, ln_ref, out_ref, bias_ref
):
    step = pl.program_id(0)
    frames, rows, cols = kv_ref.shape[1], q_ref.shape[0], q_ref.shape[1]

    @pl.when(step == 0)
    def _():
        for r in range(rows):
            bias_ref[r] = window_bias(cols_ref[...], fb_ref[...], offsets[r], cols)

    lane = lax.broadcasted_iota(jnp.int32, lp_ref.shape, 1)
    for j in range(HEADS_PER_STEP):
        part = pl.ds(j * HD, HD)
        for r in range(rows):
            near = range(max(r - 1, 0), min(r + 2, rows))
            keys = jnp.concatenate([kv_ref[0, f, n, :, part] for n in near for f in range(frames)], axis=0)
            values = jnp.concatenate([kv_ref[1, f, n, :, part] for n in near for f in range(frames)], axis=0)
            bias = bias_ref[r, :, : keys.shape[0]]
            out, level = partial_attention(q_ref[r, :, part], keys, values, bias)
            pieces = [(out, level)]
            for at, o_ref, l_ref, flag in ((0, op_ref, lp_ref, rows), (rows - 1, on_ref, ln_ref, rows + 1)):
                if r == at:
                    other = jnp.sum(
                        jnp.where(lane == step * HEADS_PER_STEP + j, l_ref[...], 0.0), axis=-1, keepdims=True
                    )
                    other = jnp.where(offsets[flag] == 1, other, NEG)
                    pieces.append((o_ref[0, :, part].astype(jnp.float32), other))
            if len(pieces) > 1:
                top = functools.reduce(jnp.maximum, [level for _, level in pieces])
                shares = [jnp.exp(level - top) for _, level in pieces]
                mixed = sum(share * piece for share, (piece, _) in zip(shares, pieces))
                out = mixed * (1.0 / sum(shares))
            out_ref[r, :, part] = out.astype(jnp.bfloat16)


def attention(queries, kv_frames, frame_mask, col_shift, place, count):
    rows, cols, wide = queries.shape
    frames = kv_frames.shape[1]
    heads = wide // HD
    step_lanes = HEADS_PER_STEP * HD
    grid = (heads // HEADS_PER_STEP,)
    first_row = place * rows
    frame_ok = jnp.concatenate([frame_mask == 1, jnp.ones((1,), dtype=bool)])
    near = min(rows, 3)
    frame_bias = jnp.tile(jnp.repeat(jnp.where(frame_ok, 0.0, NEG), cols), near)[None]
    key_cols = jnp.tile(jnp.arange(cols, dtype=jnp.int32), near * frames)[None]
    has_prev = (place > 0).astype(jnp.int32)
    has_next = (place < count - 1).astype(jnp.int32)
    own_offsets = lax.dynamic_slice_in_dim(col_shift, first_row, rows)
    total = col_shift.shape[0]
    side_rows = jnp.clip(jnp.stack([first_row - 1, first_row + rows]), 0, total - 1)
    side_offsets = col_shift[side_rows]

    q_prev = to_next(queries[rows - 1 :], "band")
    q_next = to_previous(queries[:1], "band")

    smem = pl.BlockSpec(memory_space=pltpu.SMEM)
    one = frames * cols

    def fixed(shape):
        return pl.BlockSpec(shape, lambda h: (0,) * len(shape))

    def lanes(shape, row=0):
        lead = (0,) * (len(shape) - 3)
        return pl.BlockSpec(shape, lambda h: lead + (row, 0, h))

    row_q = (1, cols, step_lanes)
    o_prev, o_next, l_prev, l_next = pl.pallas_call(
        edge_kernel,
        grid=grid,
        out_shape=(
            jax.ShapeDtypeStruct((1, cols, wide), jnp.bfloat16),
            jax.ShapeDtypeStruct((1, cols, wide), jnp.bfloat16),
            jax.ShapeDtypeStruct((cols, 128), jnp.float32),
            jax.ShapeDtypeStruct((cols, 128), jnp.float32),
        ),
        in_specs=[
            smem,
            fixed((1, one)),
            fixed((1, one)),
            lanes(row_q),
            lanes(row_q),
            lanes((2, frames, 1, cols, step_lanes), 0),
            lanes((2, frames, 1, cols, step_lanes), rows - 1),
        ],
        out_specs=(lanes(row_q), lanes(row_q), fixed((cols, 128)), fixed((cols, 128))),
        scratch_shapes=[pltpu.VMEM((2, cols, one), jnp.float32)],
        cost_estimate=pl.CostEstimate(
            flops=2 * 4 * cols * one * wide, bytes_accessed=4 * one * wide * 2, transcendentals=2 * heads * cols * one
        ),
        name="edge_attention",
    )(side_offsets, key_cols[:, :one], frame_bias[:, :one], q_prev, q_next, kv_frames, kv_frames)

    back_prev = to_next(o_next, "band")
    back_next = to_previous(o_prev, "band")
    level_prev = to_next(l_next, "band")
    level_next = to_previous(l_prev, "band")

    scalars = jnp.concatenate([own_offsets, jnp.stack([has_prev, has_next])])
    return pl.pallas_call(
        main_kernel,
        grid=grid,
        out_shape=jax.ShapeDtypeStruct(queries.shape, jnp.bfloat16),
        in_specs=[
            smem,
            fixed((1, near * one)),
            fixed((1, near * one)),
            lanes((rows, cols, step_lanes)),
            lanes((2, frames, rows, cols, step_lanes)),
            lanes(row_q),
            lanes(row_q),
            fixed((cols, 128)),
            fixed((cols, 128)),
        ],
        out_specs=lanes((rows, cols, step_lanes)),
        scratch_shapes=[pltpu.VMEM((rows, cols, near * one), jnp.float32)],
        cost_estimate=pl.CostEstimate(
            flops=4 * rows * cols * near * one * wide,
            bytes_accessed=2 * rows * one * wide * 2,
            transcendentals=rows * heads * cols * near * one,
        ),
        name="main_attention",
    )(scalars, key_cols, frame_bias, queries, kv_frames, back_prev, back_next, level_prev, level_next)


def decoder_kernel(
    group, flags, lat_ref, win_ref, wmid_ref, bin_ref, gain_ref, bmid_ref, out_ref, first_ref, act_ref
):
    width, ch = out_ref.shape[1], out_ref.shape[2]
    rows = out_ref.shape[0]
    x_at = lax.broadcasted_iota(jnp.int32, (width, ch), 0)

    @pl.loop(0, rows + 2)
    def _(i):
        source = lat_ref[i]
        left = jnp.dot(source, win_ref[0], preferred_element_type=jnp.float32)
        mid = jnp.dot(source, win_ref[1], preferred_element_type=jnp.float32)
        right = jnp.dot(source, win_ref[2], preferred_element_type=jnp.float32)
        left = jnp.where(x_at == 0, 0.0, pltpu.roll(left, 1, 0))
        right = jnp.where(x_at == width - 1, 0.0, pltpu.roll(right, width - 1, 0))
        first = left + mid + right + bin_ref[...]
        first_ref[i] = first
        scale = lax.rsqrt(jnp.mean(first * first, axis=-1, keepdims=True) + 1e-06)
        value = first * scale * gain_ref[...]
        active = value / (1.0 + jnp.exp(-value))
        outside = ((i == 0) & (flags[0] == 0)) | ((i == rows + 1) & (flags[1] == 0))
        active = jnp.where(outside, 0.0, active)
        at = pl.ds(pl.multiple_of(i * width, width), width)
        act_ref[at, 0:ch] = jnp.where(x_at == 0, 0.0, pltpu.roll(active, 1, 0)).astype(jnp.bfloat16)
        act_ref[at, ch : 2 * ch] = active.astype(jnp.bfloat16)
        act_ref[at, 2 * ch : 3 * ch] = jnp.where(
            x_at == width - 1, 0.0, pltpu.roll(active, width - 1, 0)
        ).astype(jnp.bfloat16)

    @pl.loop(0, rows // group)
    def _(g):
        total = jnp.zeros((group * width, ch), jnp.float32)
        for dy in range(3):
            at = pl.ds(pl.multiple_of((g * group + dy) * width, width), group * width)
            total += jnp.dot(
                act_ref[at, :], wmid_ref[dy * 3 * ch : (dy + 1) * 3 * ch, :], preferred_element_type=jnp.float32
            )
        total = total + bmid_ref[...]
        for y in range(group):
            here = g * group + y
            out_ref[here] = (total[y * width : (y + 1) * width] + first_ref[here + 1]).astype(jnp.bfloat16)


def decoder(latent, conv_in, bias_in, norm_gain, conv_mid, bias_mid, place, count):
    times, rows, packed = latent.shape
    ch = conv_in.shape[1]
    depth = conv_in.shape[0] // 27
    width = packed // depth
    low = to_next(latent[:, rows - 2 :], "band")
    high = to_previous(latent[:, :2], "band")
    grid_rows = jnp.concatenate([low, latent, high], axis=1)
    pixels = grid_rows.reshape(times, rows + 4, width, depth).transpose(1, 2, 0, 3)
    pixels = pixels.reshape(rows + 4, width, times * depth)
    stacked = jnp.concatenate([pixels[dy : dy + rows + 2] for dy in range(3)], axis=-1)
    weights = conv_in.reshape(3, 3, 3, depth, ch).transpose(2, 1, 0, 3, 4).reshape(3, 9 * depth, ch)
    flags = jnp.stack([(place > 0).astype(jnp.int32), (place < count - 1).astype(jnp.int32)])
    group = next(size for size in (4, 2, 1) if rows % size == 0)
    vmem = pl.BlockSpec(memory_space=pltpu.VMEM)
    return pl.pallas_call(
        functools.partial(decoder_kernel, group),
        out_shape=jax.ShapeDtypeStruct((rows, width, ch), jnp.bfloat16),
        in_specs=[pl.BlockSpec(memory_space=pltpu.SMEM)] + [vmem] * 6,
        out_specs=vmem,
        scratch_shapes=[
            pltpu.VMEM((rows + 2, width, ch), jnp.float32),
            pltpu.VMEM(((rows + 2) * width, 3 * ch), jnp.bfloat16),
        ],
        cost_estimate=pl.CostEstimate(
            flops=2 * rows * width * 9 * ch * ch, bytes_accessed=9 * ch * ch * 2, transcendentals=rows * width * ch
        ),
        name="decoder",
    )(flags, stacked, weights, conv_mid, bias_in[None], norm_gain[None], bias_mid[None])


def body(
    queries, kv_frames, frame_mask, col_shift, latent, conv_in, bias_in, norm_gain, conv_mid, bias_mid
):
    count = lax.axis_size("band")
    place = lax.axis_index("band")
    attended = attention(queries, kv_frames, frame_mask, col_shift, place, count)
    decoded = decoder(latent, conv_in, bias_in, norm_gain, conv_mid, bias_mid, place, count)
    return (attended, decoded)


def solution(mesh):
    placed = (
        P(("groups", "band"), None, None),
        P("groups", None, "band", None, None),
        P("groups"),
        P("groups"),
        P("groups", "band", None),
        P(),
        P(),
        P(),
        P(),
        P(),
    )
    return jax.shard_map(
        body,
        mesh=mesh,
        in_specs=placed,
        out_specs=(P(("groups", "band"), None, None), P(("groups", "band"), None, None)),
        check_vma=False,
    )
```

time: 534 us -> 103 us (0.19); the launches traced: 524 us -> 101 us
  local copies, waits for them, and re-layouts: 312 us -> 16.7 us
  matrix products: 121 us -> 0 us
  other arithmetic: 65.6 us -> 2.94 us
  Pallas kernels: 0 us -> 57.8 us
    dot_general x42 -> x0, matrix products: 121 us -> none  [the longest x20 90 us: attend(): jnp.einsum('bhd,fnkhd->hbfnk', query_tile, keys_tile, preferred_element_t...]
    slice x13 -> x11, local copies, waits for them, and re-layouts: 118 us -> 9.13 us  [the longest x7 5.84 us: decoder(): pixels[dy:dy + rows + 2]]
    reshape x25 -> x2, local copies, waits for them, and re-layouts: 102 us -> 1.94 us  [the longest x1 1.18 us: decoder(): grid_rows.reshape(times, rows + 4, width, depth).transpose(1, 2, 0, 3)]
    pallas_call x0 -> x3, Pallas kernels: none -> 57.8 us  [the longest x1 30.9 us: attention(): pl.pallas_call(main_kernel, grid=grid, out_shape=jax.ShapeDtypeStruct(que...]
    concatenate x31 -> x0, local copies, waits for them, and re-layouts: 30.2 us -> none  [the longest x24 19.1 us: attend(): jnp.concatenate(numerators, axis=0)]
    unnamed x217 -> x34, local copies, waits for them, and re-layouts: 26.6 us -> 2.31 us
    reduce_sum x20 -> x0, other arithmetic: 20.9 us -> none  [attend(): row_sum = jnp.sum(weights, axis=(2, 3, 4))]
    pad x2 -> x0, local copies, waits for them, and re-layouts: 20.3 us -> none  [attend(): padded = jnp.pad(window, ((0, 0), (0, 0), (0, 0), (reach, reach), (0, 0)))]
  transfers between devices with their start and end apart: 6 -> 8, of which waited for: 1 -> 0; matrix products, arithmetic and copies ran while one was open for 59% -> 15% of each run, Pallas kernels for 0% -> 13%
where the time goes in v1:
time: 103 us; the launch traced here: 101 us
  Pallas kernels  57.8 us (56%)
  starting transfers between devices  23 us (22%)
  local copies, waits for them, and re-layouts  16.7 us (16%)
  other arithmetic  2.94 us (3%)
    pallas_call x1, Pallas kernels, attention(): pl.pallas_call(main_kernel, grid=grid, out_shape=jax.ShapeDtypeStruct(que...  30.9 us
    ppermute x4, starting transfers between devices, to_next(): return lax.ppermute(block, axis, [(i, i + 1) for i in range(count - 1)])  14.7 us
    pallas_call x1, Pallas kernels, attention(): pl.pallas_call(edge_kernel, grid=grid, out_shape=(jax.ShapeDtypeStruct((1...  13.9 us
    pallas_call x1, Pallas kernels, decoder(): pl.pallas_call(functools.partial(decoder_kernel, group), out_shape=jax.Sh...  13.1 us
    ppermute x4, starting transfers between devices, to_previous(): return lax.ppermute(block, axis, [(i + 1, i) for i in range(count - 1)])  8.28 us
    slice x7, local copies, waits for them, and re-layouts, decoder(): pixels[dy:dy + rows + 2]  5.84 us
    unnamed x34, local copies, waits for them, and re-layouts  2.31 us
    slice x1, local copies, waits for them, and re-layouts, attention(): q_next = to_previous(queries[:1], 'band')  2.15 us
  transfers between devices with their start and end apart: 8, of which 0 were waited for; matrix products, arithmetic and copies ran while one was open for 15% of the time, Pallas kernels for 13%

profile of v1, /device:TPU:21, one launch (start us, length us, event | category | flops | bytes accessed | tf_op | source)
XLA Modules:
  0.0 101.4 jit_solution(5331580766627760800)
XLA Ops:
  0.6 0.0 copy-start.6
  0.6 0.0 copy-start
  0.7 0.0 copy-start.16
  0.7 0.0 copy-start.5
  0.7 0.0 copy-start.11
  0.7 0.0 copy-start.12
  0.7 0.0 copy-start.13
  0.7 2.2 %fusion.1 = (bf16[1,80,2560]{2,1,0:T(8,128)(2,1)}, bf16[1,80,2560]{2,1,0:T(8,128)(2,1)}) fusion(bf16[4,80,2560]{2,1,0:T(8,128)(2,1)} %q_ref.1), kind=kLoop, calls=%fused_computation.11 | loop fusion | bytes 1638400 | tf_op jit(solution)/shard_map/slice | solution.py:127
  2.9 3.7 %collective-permute-start = (bf16[1,80,2560]{2,1,0:T(8,128)(2,1)}, bf16[1,80,2560]{2,1,0:T(8,128)(2,1)S(1)}, u32[]{:S(2)}, u32[]{:S(2)}) collective-permute-start(bf16[1,80,2560]{2,1,0:T(8,128)(2,1)} %get-tuple-element.11), channel_id=1, source_target_pairs={{0,1},{1,2},{2,3},{3,4},{4,5},{5,6},{6,7},{7,8},{8,9},{9,10},{10,1... | collective-permute-start | bytes 1228808 | tf_op jit(solution)/shard_map/ppermute | solution.py:20
  6.6 1.9 %collective-permute-start.1 = (bf16[1,80,2560]{2,1,0:T(8,128)(2,1)}, bf16[1,80,2560]{2,1,0:T(8,128)(2,1)}, u32[]{:S(2)}, u32[]{:S(2)}) collective-permute-start(bf16[1,80,2560]{2,1,0:T(8,128)(2,1)} %get-tuple-element.10), channel_id=1, source_target_pairs={{1,0},{2,1},{3,2},{4,3},{5,4},{6,5},{7,6},{8,7},{9,8},{10,9},{11,1... | collective-permute-start | bytes 1228808 | tf_op jit(solution)/shard_map/ppermute | solution.py:25
  8.5 0.0 copy-done.6
  8.6 2.5 %collective-permute-start.7 = (bf16[3,2,2560]{2,1,0:T(2,128)(2,1)S(1)}, bf16[3,2,2560]{2,1,0:T(2,128)(2,1)S(1)}, u32[]{:S(2)}, u32[]{:S(2)}) collective-permute-start(bf16[3,2,2560]{2,1,0:T(2,128)(2,1)S(1)} %get-tuple-element.16), channel_id=1, source_target_pairs={{1,0},{2,1},{3,2},{4,3},{5,4},{6,5},{7,6},{8,7},{9,8},{10,9},{11,1... | collective-permute-start | bytes 92168 | tf_op jit(solution)/shard_map/ppermute | solution.py:25
  11.1 3.9 %collective-permute-start.6 = (bf16[3,2,2560]{2,1,0:T(2,128)(2,1)S(1)}, bf16[3,2,2560]{2,1,0:T(2,128)(2,1)S(1)}, u32[]{:S(2)}, u32[]{:S(2)}) collective-permute-start(bf16[3,2,2560]{2,1,0:T(2,128)(2,1)S(1)} %get-tuple-element.15), channel_id=1, source_target_pairs={{0,1},{1,2},{2,3},{3,4},{4,5},{5,6},{6,7},{7,8},{8,9},{9,10},{10,1... | collective-permute-start | bytes 92168 | tf_op jit(solution)/shard_map/ppermute | solution.py:20
  15.0 0.0 copy-done
  15.0 0.1 dynamic_slice.3
  15.1 0.6 pad_add_fusion.1.flags
  15.7 0.6 pad_add_fusion.offsets
  16.3 0.1 fusion
  16.4 0.1 add_select_fusion
  16.5 0.1 broadcast_in_dim_tile.8.cols_ref
  16.6 0.1 broadcast_in_dim.23
  16.6 0.1 tile.16
  16.7 0.1 broadcast_in_dim_tile.9.fb_ref
  16.8 1.2 %gather_fusion = s32[2]{0:T(128)} fusion(s32[64]{0:T(128)S(1)} %copy-done, s32[1024]{0:T(1024)S(1)} %pad_clamp_fusion), kind=kCustom, calls=%fused_computation | custom fusion | bytes 24 | tf_op jit(solution)/shard_map/gather | solution.py:124
  18.0 0.5 slice.50.cols_ref
  18.6 0.5 slice.51.fb_ref
  19.1 0.8 copy.20
  19.9 0.0 copy-done.11
  19.9 0.6 broadcast_in_dim.24.bin_ref
  20.5 0.6 broadcast_in_dim.25.gain_ref
  21.0 0.6 broadcast_in_dim.26.bmid_ref
  21.6 0.0 collective-permute-done.7
  21.6 0.0 collective-permute-done.6
  21.6 0.1 pad_maximum_fusion.1
  21.7 1.2 %reshape.58 = bf16[3,12,160,16]{3,2,1,0:T(8,128)(2,1)S(1)} reshape(bf16[3,12,2560]{2,1,0:T(8,128)(2,1)S(1)} %pad_maximum_fusion.1) | data formatting | bytes 368640 | tf_op jit(solution)/shard_map/reshape | solution.py:249
  22.9 2.0 %fusion.2 = (bf16[10,160,3,16]{3,1,0,2:T(8,128)(2,1)S(1)}, bf16[10,160,3,16]{3,1,0,2:T(8,128)(2,1)}, bf16[10,160,3,16]{3,1,0,2:T(8,128)(2,1)}) fusion(bf16[12,160,3,16]{3,1,0,2:T(8,128)(2,1)S(1)} %bitcast.14), kind=kLoop, calls=%fused_computation.12 | loop fusion | bytes 921600 | tf_op jit(solution)/shard_map/slice | solution.py:251
  25.0 1.9 %copy.16 = bf16[10,160,3,16]{1,3,2,0:T(8,128)(2,1)S(1)} copy(bf16[10,160,3,16]{3,1,0,2:T(8,128)(2,1)} %get-tuple-element.13) | data formatting | bytes 307200 | tf_op jit(solution)/shard_map/slice | solution.py:251
  26.9 0.3 copy.19
  27.2 0.5 copy.15
  27.7 0.3 copy.18
  28.0 0.6 copy.14
  28.5 0.3 copy.17
  28.8 0.0 collective-permute-done.qp_ref
  28.8 0.0 copy-start.2
  28.8 0.0 collective-permute-done.1.qn_ref
  28.8 0.7 copy-done.2
  29.6 13.9 %edge_attention.1 = (bf16[1,80,2560]{2,1,0:T(8,128)(2,1)}, bf16[1,80,2560]{2,1,0:T(8,128)(2,1)}, f32[80,128]{1,0:T(8,128)}, f32[80,128]{1,0:T(8,128)}) custom-call(s32[2]{0:T(128)} %gather_fusion, s32[1,320]{1,0:T(1,128)} %slice.50.cols_ref, f32[1,320]{1,0:T(1,128)} %slice.51.fb_ref, bf16[1,80,2560]{2,1,0:T(8,128)(2,1)} %copy-done.2, ...), custom_call_target="tpu_custom_call" | custom-call | flops 524288000 | bytes 6553600 | tf_op jit(solution)/shard_map/edge_attention/pallas_call | solution.py:140
  43.4 0.0 copy-start.14
  43.4 2.5 %collective-permute-start.2 = (bf16[1,80,2560]{2,1,0:T(8,128)(2,1)}, bf16[1,80,2560]{2,1,0:T(8,128)(2,1)S(1)}, u32[]{:S(2)}, u32[]{:S(2)}) collective-permute-start(bf16[1,80,2560]{2,1,0:T(8,128)(2,1)} %get-tuple-element.6), channel_id=1, source_target_pairs={{0,1},{1,2},{2,3},{3,4},{4,5},{5,6},{6,7},{7,8},{8,9},{9,10},{10,1... | collective-permute-start | bytes 1228808 | tf_op jit(solution)/shard_map/ppermute | solution.py:20
  46.0 1.9 %collective-permute-start.3 = (bf16[1,80,2560]{2,1,0:T(8,128)(2,1)}, bf16[1,80,2560]{2,1,0:T(8,128)(2,1)S(1)}, u32[]{:S(2)}, u32[]{:S(2)}) collective-permute-start(bf16[1,80,2560]{2,1,0:T(8,128)(2,1)} %get-tuple-element.7), channel_id=1, source_target_pairs={{1,0},{2,1},{3,2},{4,3},{5,4},{6,5},{7,6},{8,7},{9,8},{10,9},{11,1... | collective-permute-start | bytes 1228808 | tf_op jit(solution)/shard_map/ppermute | solution.py:25
  47.9 1.5 %pad_maximum_fusion.lat_ref = bf16[10,160,144]{2,1,0:T(8,128)(2,1)} fusion(bf16[10,160,48]{2,1,0:T(8,128)(2,1)S(1)} %copy.19, bf16[10,160,48]{2,1,0:T(8,128)(2,1)S(1)} %copy.18, bf16[10,160,48]{2,1,0:T(8,128)(2,1)S(1)} %copy.17), kind=kLoop, calls=%fused_computation.1 | loop fusion | flops 1382400 | bytes 921600 | tf_op jit(solution)/shard_map/concatenate | solution.py:251
  49.4 0.0 copy-done.15
  49.4 4.5 %collective-permute-start.4 = (f32[80,128]{1,0:T(8,128)S(1)}, f32[80,128]{1,0:T(8,128)S(1)}, u32[]{:S(2)}, u32[]{:S(2)}) collective-permute-start(f32[80,128]{1,0:T(8,128)S(1)} %copy-done.15), channel_id=1, source_target_pairs={{0,1},{1,2},{2,3},{3,4},{4,5},{5,6},{6,7},{7,8},{8,9},{9,10},{10,1... | collective-permute-start | bytes 122888 | tf_op jit(solution)/shard_map/ppermute | solution.py:20
  54.0 1.9 %collective-permute-start.5 = (f32[80,128]{1,0:T(8,128)S(1)}, f32[80,128]{1,0:T(8,128)S(1)}, u32[]{:S(2)}, u32[]{:S(2)}) collective-permute-start(f32[80,128]{1,0:T(8,128)S(1)} %copy-done.14), channel_id=1, source_target_pairs={{1,0},{2,1},{3,2},{4,3},{5,4},{6,5},{7,6},{8,7},{9,8},{10,9},{11,1... | collective-permute-start | bytes 122888 | tf_op jit(solution)/shard_map/ppermute | solution.py:25
  55.9 13.1 %decoder.1 = bf16[8,160,384]{2,1,0:T(8,128)(2,1)} custom-call(s32[2]{0:T(128)} %pad_add_fusion.1.flags, bf16[10,160,144]{2,1,0:T(8,128)(2,1)} %pad_maximum_fusion.lat_ref, bf16[3,144,384]{2,1,0:T(8,128)(2,1)} %bitcast.19, bf16[3456,384]{1,0:T(8,128)(2,1)} %wmid_ref.1, f32[1,384]{1,0:T(1,128)} %broadcast_in_dim.24.bin_ref, ...), custom_call_target="tpu_custom_call" | custom-call | flops 3397386240 | bytes 2654208 | tf_op jit(solution)/shard_map/decoder/pallas_call | solution.py:256
  69.0 0.0 collective-permute-done.4.lp_ref
  69.0 0.0 collective-permute-done.5.ln_ref
  69.0 0.0 collective-permute-done.2.op_ref
  69.0 0.0 collective-permute-done.3.on_ref
  69.0 0.6 copy-done.7
  69.6 0.0 copy-done.8
  69.6 0.2 copy-done.3
  69.8 0.8 copy-done.4
  70.6 30.9 %main_attention.1 = bf16[4,80,2560]{2,1,0:T(8,128)(2,1)} custom-call(s32[6]{0:T(128)} %pad_add_fusion.offsets, s32[1,960]{1,0:T(1,128)} %copy-done.9, f32[1,960]{1,0:T(1,128)} %copy-done.10, bf16[4,80,2560]{2,1,0:T(8,128)(2,1)} %q_ref.1, bf16[2,4,4,80,2560]{4,3,2,1,0:T(8,128)(2,1)} %kv_ref.1, bf16[1,80,2560]{2,1,0:T(8,128)(2,1)} %copy-done.3, ...), custom_call_target="tpu_custom_call" | custom-call | flops 3145728000 | bytes 13107200 | tf_op jit(solution)/shard_map/main_attention/pallas_call | solution.py:172
  (21 shorter events, 0.1 us)
Async XLA Ops:
  0.6 7.9 %copy-start.6 = (bf16[3,8,2560]{2,1,0:T(8,128)(2,1)S(1)}, bf16[3,8,2560]{2,1,0:T(8,128)(2,1)}, u32[]{:S(2)}) copy-start(bf16[3,8,2560]{2,1,0:T(8,128)(2,1)} %param.14) | copy-start | bytes 368644
  0.6 14.4 %copy-start = (s32[64]{0:T(128)S(1)}, s32[64]{0:T(128)}, u32[]{:S(2)}) copy-start(s32[64]{0:T(128)} %param.13) | copy-start | bytes 772
  0.7 15.6 %copy-start.16 = (s32[3]{0:T(128)S(1)}, s32[3]{0:T(128)}, u32[]{:S(2)}) copy-start(s32[3]{0:T(128)} %param.12) | copy-start | bytes 40
  0.7 18.4 %copy-start.5 = (bf16[432,384]{1,0:T(8,128)(2,1)S(1)}, bf16[432,384]{1,0:T(8,128)(2,1)}, u32[]{:S(2)}) copy-start(bf16[432,384]{1,0:T(8,128)(2,1)} %param.15) | copy-start | bytes 995332
  0.7 19.2 %copy-start.11 = (f32[384]{0:T(512)S(1)}, f32[384]{0:T(512)}, u32[]{:S(2)}) copy-start(f32[384]{0:T(512)} %param.16) | copy-start | bytes 4612
  0.7 19.8 %copy-start.12 = (f32[384]{0:T(512)S(1)}, f32[384]{0:T(512)}, u32[]{:S(2)}) copy-start(f32[384]{0:T(512)} %param.17) | copy-start | bytes 4612
  0.7 20.3 %copy-start.13 = (f32[384]{0:T(512)S(1)}, f32[384]{0:T(512)}, u32[]{:S(2)}) copy-start(f32[384]{0:T(512)} %param.19) | copy-start | bytes 4612
  2.9 25.9 %collective-permute-start = (bf16[1,80,2560]{2,1,0:T(8,128)(2,1)}, bf16[1,80,2560]{2,1,0:T(8,128)(2,1)S(1)}, u32[]{:S(2)}, u32[]{:S(2)}) collective-permute-start(bf16[1,80,2560]{2,1,0:T(8,128)(2,1)} %get-tuple-element.11), channel_id=1, source_target_pairs={{0,1},{1,2},{2,3},{3,4},{4,5},{5,6},{6,7},{7,8},{8,9},{9,10},{10,1... | collective-permute-start | bytes 1228808 | tf_op jit(solution)/shard_map/ppermute | solution.py:20
  6.6 22.3 %collective-permute-start.1 = (bf16[1,80,2560]{2,1,0:T(8,128)(2,1)}, bf16[1,80,2560]{2,1,0:T(8,128)(2,1)}, u32[]{:S(2)}, u32[]{:S(2)}) collective-permute-start(bf16[1,80,2560]{2,1,0:T(8,128)(2,1)} %get-tuple-element.10), channel_id=1, source_target_pairs={{1,0},{2,1},{3,2},{4,3},{5,4},{6,5},{7,6},{8,7},{9,8},{10,9},{11,1... | collective-permute-start | bytes 1228808 | tf_op jit(solution)/shard_map/ppermute | solution.py:25
  8.6 13.1 %collective-permute-start.7 = (bf16[3,2,2560]{2,1,0:T(2,128)(2,1)S(1)}, bf16[3,2,2560]{2,1,0:T(2,128)(2,1)S(1)}, u32[]{:S(2)}, u32[]{:S(2)}) collective-permute-start(bf16[3,2,2560]{2,1,0:T(2,128)(2,1)S(1)} %get-tuple-element.16), channel_id=1, source_target_pairs={{1,0},{2,1},{3,2},{4,3},{5,4},{6,5},{7,6},{8,7},{9,8},{10,9},{11,1... | collective-permute-start | bytes 92168 | tf_op jit(solution)/shard_map/ppermute | solution.py:25
  11.1 10.5 %collective-permute-start.6 = (bf16[3,2,2560]{2,1,0:T(2,128)(2,1)S(1)}, bf16[3,2,2560]{2,1,0:T(2,128)(2,1)S(1)}, u32[]{:S(2)}, u32[]{:S(2)}) collective-permute-start(bf16[3,2,2560]{2,1,0:T(2,128)(2,1)S(1)} %get-tuple-element.15), channel_id=1, source_target_pairs={{0,1},{1,2},{2,3},{3,4},{4,5},{5,6},{6,7},{7,8},{8,9},{9,10},{10,1... | collective-permute-start | bytes 92168 | tf_op jit(solution)/shard_map/ppermute | solution.py:20
  16.5 6.4 %copy-start.9 = (s32[1,960]{1,0:T(1,128)}, s32[1,960]{1,0:T(1,128)S(1)}, u32[]{:S(2)}) copy-start(s32[1,960]{1,0:T(1,128)S(1)} %broadcast_in_dim_tile.8.cols_ref) | copy-start | bytes 11524
  16.8 6.1 %copy-start.10 = (f32[1,960]{1,0:T(1,128)}, f32[1,960]{1,0:T(1,128)S(1)}, u32[]{:S(2)}) copy-start(f32[1,960]{1,0:T(1,128)S(1)} %broadcast_in_dim_tile.9.fb_ref) | copy-start | bytes 11524
  25.0 2.2 %copy-start.1 = (bf16[10,160,3,16]{3,1,0,2:T(8,128)(2,1)S(1)}, bf16[10,160,3,16]{3,1,0,2:T(8,128)(2,1)}, u32[]{:S(2)}) copy-start(bf16[10,160,3,16]{3,1,0,2:T(8,128)(2,1)} %get-tuple-element.14) | copy-start | bytes 460804
  28.8 0.8 copy-start.2
  43.4 6.0 %copy-start.15 = (f32[80,128]{1,0:T(8,128)S(1)}, f32[80,128]{1,0:T(8,128)}, u32[]{:S(2)}) copy-start(f32[80,128]{1,0:T(8,128)} %get-tuple-element.8) | copy-start | bytes 122884
  43.4 10.5 %copy-start.14 = (f32[80,128]{1,0:T(8,128)S(1)}, f32[80,128]{1,0:T(8,128)}, u32[]{:S(2)}) copy-start(f32[80,128]{1,0:T(8,128)} %get-tuple-element.9) | copy-start | bytes 122884
  43.4 25.6 %collective-permute-start.2 = (bf16[1,80,2560]{2,1,0:T(8,128)(2,1)}, bf16[1,80,2560]{2,1,0:T(8,128)(2,1)S(1)}, u32[]{:S(2)}, u32[]{:S(2)}) collective-permute-start(bf16[1,80,2560]{2,1,0:T(8,128)(2,1)} %get-tuple-element.6), channel_id=1, source_target_pairs={{0,1},{1,2},{2,3},{3,4},{4,5},{5,6},{6,7},{7,8},{8,9},{9,10},{10,1... | collective-permute-start | bytes 1228808 | tf_op jit(solution)/shard_map/ppermute | solution.py:20
  46.0 23.0 %collective-permute-start.3 = (bf16[1,80,2560]{2,1,0:T(8,128)(2,1)}, bf16[1,80,2560]{2,1,0:T(8,128)(2,1)S(1)}, u32[]{:S(2)}, u32[]{:S(2)}) collective-permute-start(bf16[1,80,2560]{2,1,0:T(8,128)(2,1)} %get-tuple-element.7), channel_id=1, source_target_pairs={{1,0},{2,1},{3,2},{4,3},{5,4},{6,5},{7,6},{8,7},{9,8},{10,9},{11,1... | collective-permute-start | bytes 1228808 | tf_op jit(solution)/shard_map/ppermute | solution.py:25
  49.4 19.6 %collective-permute-start.4 = (f32[80,128]{1,0:T(8,128)S(1)}, f32[80,128]{1,0:T(8,128)S(1)}, u32[]{:S(2)}, u32[]{:S(2)}) collective-permute-start(f32[80,128]{1,0:T(8,128)S(1)} %copy-done.15), channel_id=1, source_target_pairs={{0,1},{1,2},{2,3},{3,4},{4,5},{5,6},{6,7},{7,8},{8,9},{9,10},{10,1... | collective-permute-start | bytes 122888 | tf_op jit(solution)/shard_map/ppermute | solution.py:20
  54.0 15.0 %collective-permute-start.5 = (f32[80,128]{1,0:T(8,128)S(1)}, f32[80,128]{1,0:T(8,128)S(1)}, u32[]{:S(2)}, u32[]{:S(2)}) collective-permute-start(f32[80,128]{1,0:T(8,128)S(1)} %copy-done.14), channel_id=1, source_target_pairs={{1,0},{2,1},{3,2},{4,3},{5,4},{6,5},{7,6},{8,7},{9,8},{10,9},{11,1... | collective-permute-start | bytes 122888 | tf_op jit(solution)/shard_map/ppermute | solution.py:25
  69.0 0.6 copy-start.7
  69.0 0.6 copy-start.8
  69.0 0.8 copy-start.3
  69.8 0.8 copy-start.4

commit v2 on v1

v2 whole, which is shorter than its diff:
```python
import functools
import math

import jax
import jax.numpy as jnp
from jax import lax
from jax.experimental import pallas as pl
from jax.experimental.pallas import tpu as pltpu
from jax.sharding import PartitionSpec as P

HD = 128
RC = 8
NEG = -1e30
SCALE = 1.0 / math.sqrt(HD)
HEADS_PER_STEP = 4


def to_next(block, axis):
    count = lax.axis_size(axis)
    return lax.ppermute(block, axis, [(i, i + 1) for i in range(count - 1)])


def to_previous(block, axis):
    count = lax.axis_size(axis)
    return lax.ppermute(block, axis, [(i + 1, i) for i in range(count - 1)])


def fill_bias(store, copies, offset, mask, cols, frames):
    key = lax.broadcasted_iota(jnp.int32, (cols, cols), 1)
    query = lax.broadcasted_iota(jnp.int32, (cols, cols), 0)
    ok = jnp.abs(key - query - offset) <= RC
    for f in range(frames):
        open_value = jnp.where(mask[f] == 1, 0.0, NEG) if f < frames - 1 else 0.0
        piece = jnp.where(ok, open_value, NEG)
        for n in range(copies):
            at = (n * frames + f) * cols
            store(at, piece)


def score(query, keys):
    return lax.dot_general(
        query, keys, (((1,), (1,)), ((), ())), preferred_element_type=jnp.float32
    )


def soften(scores, bias):
    scores = scores + bias
    top = jnp.max(scores, axis=-1, keepdims=True)
    weights = jnp.exp((scores - top) * SCALE)
    total = jnp.sum(weights, axis=-1, keepdims=True)
    return weights.astype(jnp.bfloat16), total, top * SCALE + jnp.log(total)


def run_staggered(tasks):
    ahead = tasks[0][0]()
    for at, (_, biases, values, finish) in enumerate(tasks):
        scores = ahead
        if at + 1 < len(tasks):
            ahead = tasks[at + 1][0]()
        weights, total, level = soften(scores, biases())
        numerator = jnp.dot(weights, values(), preferred_element_type=jnp.float32)
        finish(numerator * (1.0 / total), level)


def stack_rows(kv_ref, which, rows, part):
    return jnp.concatenate(
        [kv_ref[which, f, n, :, part] for n in rows for f in range(kv_ref.shape[1])], axis=0
    )


def edge_kernel(
    total_rows, rows, shift_ref, mask_ref, qp_ref, qn_ref, kvf_ref, kvl_ref, op_ref, on_ref, bias_ref, level_ref
):
    step = pl.program_id(0)
    frames, cols = kvf_ref.shape[1], kvf_ref.shape[3]
    wide = op_ref.shape[1] - 3 * 128

    @pl.when(step == 0)
    def _():
        first_row = lax.axis_index("band") * rows
        sides = (jnp.maximum(first_row - 1, 0), jnp.minimum(first_row + rows, total_rows - 1))
        for side, row in enumerate(sides):

            def store(at, piece, side=side):
                bias_ref[side, :, at : at + cols] = piece

            fill_bias(store, 1, shift_ref[row], mask_ref, cols, frames)
        level_ref[...] = jnp.zeros_like(level_ref)

    lane = lax.broadcasted_iota(jnp.int32, (cols, 128), 1)
    tasks = []
    for side, (q_ref, kv_ref, o_ref) in enumerate(((qp_ref, kvf_ref, op_ref), (qn_ref, kvl_ref, on_ref))):
        for j in range(HEADS_PER_STEP):
            part = pl.ds(j * HD, HD)
            head = step * HEADS_PER_STEP + j

            def finish(out, level, side=side, head=head, o_ref=o_ref):
                o_ref[:, pl.ds(pl.multiple_of(head * HD, HD), HD)] = out.astype(jnp.bfloat16)
                level_ref[side] = jnp.where(lane == head, level, level_ref[side])

            tasks.append((
                lambda q_ref=q_ref, kv_ref=kv_ref, part=part: score(q_ref[:, part], stack_rows(kv_ref, 0, (0,), part)),
                lambda side=side: bias_ref[side],
                lambda kv_ref=kv_ref, part=part: stack_rows(kv_ref, 1, (0,), part),
                finish,
            ))
    run_staggered(tasks)

    @pl.when(step == pl.num_programs(0) - 1)
    def _():
        for side, o_ref in enumerate((op_ref, on_ref)):
            rest = level_ref[side]
            for k in range(3):
                piece = rest.astype(jnp.bfloat16)
                o_ref[:, wide + k * 128 : wide + (k + 1) * 128] = piece
                rest = rest - piece.astype(jnp.float32)


def main_kernel(shift_ref, mask_ref, q_ref, kv_ref, op_ref, on_ref, out_ref, bias_ref):
    step = pl.program_id(0)
    place = lax.axis_index("band")
    count = lax.axis_size("band")
    frames, rows, cols = kv_ref.shape[1], q_ref.shape[0], q_ref.shape[1]
    wide = op_ref.shape[1] - 3 * 128

    @pl.when(step == 0)
    def _():
        for r in range(rows):

            def store(at, piece, r=r):
                bias_ref[r, :, at : at + cols] = piece

            fill_bias(store, min(rows, 3), shift_ref[place * rows + r], mask_ref, cols, frames)

    lane = lax.broadcasted_iota(jnp.int32, (cols, 128), 1)
    tasks = []
    for j in range(HEADS_PER_STEP):
        part = pl.ds(j * HD, HD)
        head = step * HEADS_PER_STEP + j
        for r in range(rows):
            near = tuple(range(max(r - 1, 0), min(r + 2, rows)))
            span = len(near) * frames * cols

            def finish(out, level, r=r, part=part, head=head):
                pieces = [(out, level)]
                for at, o_ref, there in ((0, op_ref, place > 0), (rows - 1, on_ref, place < count - 1)):
                    if r == at:
                        other = sum(
                            o_ref[:, wide + k * 128 : wide + (k + 1) * 128].astype(jnp.float32) for k in range(3)
                        )
                        other = jnp.sum(jnp.where(lane == head, other, 0.0), axis=-1, keepdims=True)
                        other = jnp.where(there, other, NEG)
                        piece = o_ref[:, pl.ds(pl.multiple_of(head * HD, HD), HD)]
                        pieces.append((piece.astype(jnp.float32), other))
                if len(pieces) > 1:
                    top = functools.reduce(jnp.maximum, [level for _, level in pieces])
                    shares = [jnp.exp(level - top) for _, level in pieces]
                    mixed = sum(share * piece for share, (piece, _) in zip(shares, pieces))
                    out = mixed * (1.0 / sum(shares))
                out_ref[r, :, part] = out.astype(jnp.bfloat16)

            tasks.append((
                lambda r=r, near=near, part=part: score(q_ref[r, :, part], stack_rows(kv_ref, 0, near, part)),
                lambda r=r, span=span: bias_ref[r, :, :span],
                lambda near=near, part=part: stack_rows(kv_ref, 1, near, part),
                finish,
            ))
    run_staggered(tasks)


def attention(queries, kv_frames, frame_mask, col_shift, q_prev, q_next):
    rows, cols, wide = queries.shape
    frames = kv_frames.shape[1]
    heads = wide // HD
    step_lanes = HEADS_PER_STEP * HD
    grid = (heads // HEADS_PER_STEP,)
    near = min(rows, 3)
    smem = pl.BlockSpec(memory_space=pltpu.SMEM)
    one = frames * cols
    packed = wide + 3 * 128

    def fixed(shape):
        return pl.BlockSpec(shape, lambda h: (0,) * len(shape))

    def lanes(shape, row=0):
        lead = (0,) * (len(shape) - 3)
        return pl.BlockSpec(shape, lambda h: lead + (row, 0, h))

    row_q = pl.BlockSpec((cols, step_lanes), lambda h: (0, h))
    o_prev, o_next = pl.pallas_call(
        functools.partial(edge_kernel, col_shift.shape[0], rows),
        grid=grid,
        out_shape=(jax.ShapeDtypeStruct((cols, packed), jnp.bfloat16),) * 2,
        in_specs=[
            smem,
            smem,
            row_q,
            row_q,
            lanes((2, frames, 1, cols, step_lanes), 0),
            lanes((2, frames, 1, cols, step_lanes), rows - 1),
        ],
        out_specs=(fixed((cols, packed)),) * 2,
        scratch_shapes=[pltpu.VMEM((2, cols, one), jnp.float32), pltpu.VMEM((2, cols, 128), jnp.float32)],
        cost_estimate=pl.CostEstimate(
            flops=2 * 4 * cols * one * wide, bytes_accessed=4 * one * wide * 2, transcendentals=2 * heads * cols * one
        ),
        name="edge_attention",
    )(col_shift, frame_mask, q_prev, q_next, kv_frames, kv_frames)

    back_prev = to_next(o_next, "band")
    back_next = to_previous(o_prev, "band")

    return pl.pallas_call(
        main_kernel,
        grid=grid,
        out_shape=jax.ShapeDtypeStruct(queries.shape, jnp.bfloat16),
        in_specs=[
            smem,
            smem,
            lanes((rows, cols, step_lanes)),
            lanes((2, frames, rows, cols, step_lanes)),
            fixed((cols, packed)),
            fixed((cols, packed)),
        ],
        out_specs=lanes((rows, cols, step_lanes)),
        scratch_shapes=[pltpu.VMEM((rows, cols, near * one), jnp.float32)],
        cost_estimate=pl.CostEstimate(
            flops=4 * rows * cols * near * one * wide,
            bytes_accessed=2 * rows * one * wide * 2,
            transcendentals=rows * heads * cols * near * one,
        ),
        name="main_attention",
    )(col_shift, frame_mask, queries, kv_frames, back_prev, back_next)


def decoder_kernel(
    group, lat_ref, cin_ref, wmid_ref, bin_ref, gain_ref, bmid_ref, out_ref, win_ref, first_ref, act_ref
):
    place = lax.axis_index("band")
    count = lax.axis_size("band")
    depth = cin_ref.shape[0] // 27
    for dx in range(3):
        for dy in range(3):
            for dt in range(3):
                source_at = ((dt * 3 + dy) * 3 + dx) * depth
                at = (dy * 3 + dt) * depth
                win_ref[dx, at : at + depth] = cin_ref[source_at : source_at + depth]
    width, ch = out_ref.shape[1], out_ref.shape[2]
    rows = out_ref.shape[0]
    x_at = lax.broadcasted_iota(jnp.int32, (width, ch), 0)

    @pl.loop(0, rows + 2)
    def _(i):
        source = lat_ref[i]
        left = jnp.dot(source, win_ref[0], preferred_element_type=jnp.float32)
        mid = jnp.dot(source, win_ref[1], preferred_element_type=jnp.float32)
        right = jnp.dot(source, win_ref[2], preferred_element_type=jnp.float32)
        left = jnp.where(x_at == 0, 0.0, pltpu.roll(left, 1, 0))
        right = jnp.where(x_at == width - 1, 0.0, pltpu.roll(right, width - 1, 0))
        first = left + mid + right + bin_ref[...][None]
        first_ref[i] = first
        scale = lax.rsqrt(jnp.mean(first * first, axis=-1, keepdims=True) + 1e-06)
        value = first * scale * gain_ref[...][None]
        active = value / (1.0 + jnp.exp(-value))
        outside = ((i == 0) & (place == 0)) | ((i == rows + 1) & (place == count - 1))
        active = jnp.where(outside, 0.0, active)
        at = pl.ds(pl.multiple_of(i * width, width), width)
        act_ref[at, 0:ch] = jnp.where(x_at == 0, 0.0, pltpu.roll(active, 1, 0)).astype(jnp.bfloat16)
        act_ref[at, ch : 2 * ch] = active.astype(jnp.bfloat16)
        act_ref[at, 2 * ch : 3 * ch] = jnp.where(
            x_at == width - 1, 0.0, pltpu.roll(active, width - 1, 0)
        ).astype(jnp.bfloat16)

    @pl.loop(0, rows // group)
    def _(g):
        total = jnp.zeros((group * width, ch), jnp.float32)
        for dy in range(3):
            at = pl.ds(pl.multiple_of((g * group + dy) * width, width), group * width)
            total += jnp.dot(
                act_ref[at, :], wmid_ref[dy * 3 * ch : (dy + 1) * 3 * ch, :], preferred_element_type=jnp.float32
            )
        total = total + bmid_ref[...][None]
        for y in range(group):
            here = g * group + y
            out_ref[here] = (total[y * width : (y + 1) * width] + first_ref[here + 1]).astype(jnp.bfloat16)


def decoder(latent, conv_in, bias_in, norm_gain, conv_mid, bias_mid, low, high):
    times, rows, packed = latent.shape
    ch = conv_in.shape[1]
    depth = conv_in.shape[0] // 27
    width = packed // depth
    grid_rows = jnp.concatenate([low, latent, high], axis=1)
    pixels = grid_rows.reshape(times, rows + 4, width, depth).transpose(1, 2, 0, 3)
    pixels = pixels.reshape(rows + 4, width, times * depth)
    stacked = jnp.concatenate([pixels[dy : dy + rows + 2] for dy in range(3)], axis=-1)
    group = next(size for size in (4, 2, 1) if rows % size == 0)
    vmem = pl.BlockSpec(memory_space=pltpu.VMEM)
    return pl.pallas_call(
        functools.partial(decoder_kernel, group),
        out_shape=jax.ShapeDtypeStruct((rows, width, ch), jnp.bfloat16),
        in_specs=[vmem] * 6,
        out_specs=vmem,
        scratch_shapes=[
            pltpu.VMEM((3, 9 * depth, ch), jnp.bfloat16),
            pltpu.VMEM((rows + 2, width, ch), jnp.float32),
            pltpu.VMEM(((rows + 2) * width, 3 * ch), jnp.bfloat16),
        ],
        cost_estimate=pl.CostEstimate(
            flops=2 * rows * width * 9 * ch * ch, bytes_accessed=9 * ch * ch * 2, transcendentals=rows * width * ch
        ),
        name="decoder",
    )(stacked, conv_in, conv_mid, bias_in, norm_gain, bias_mid)


def body(
    queries, kv_frames, frame_mask, col_shift, latent, conv_in, bias_in, norm_gain, conv_mid, bias_mid
):
    rows, cols, wide = queries.shape
    times, lat_rows, lat_wide = latent.shape
    low_rows = latent[:, lat_rows - 2 :].reshape(times * 2, lat_wide)
    high_rows = latent[:, :2].reshape(times * 2, lat_wide)
    low = to_next(jnp.concatenate([queries[rows - 1], low_rows]), "band")
    high = to_previous(jnp.concatenate([queries[0], high_rows]), "band")
    attended = attention(queries, kv_frames, frame_mask, col_shift, low, high)
    low_rows = low[cols:].reshape(times, 2, lat_wide)
    high_rows = high[cols:].reshape(times, 2, lat_wide)
    decoded = decoder(latent, conv_in, bias_in, norm_gain, conv_mid, bias_mid, low_rows, high_rows)
    return (attended, decoded)


def solution(mesh):
    placed = (
        P(("groups", "band"), None, None),
        P("groups", None, "band", None, None),
        P("groups"),
        P("groups"),
        P("groups", "band", None),
        P(),
        P(),
        P(),
        P(),
        P(),
    )
    return jax.shard_map(
        body,
        mesh=mesh,
        in_specs=placed,
        out_specs=(P(("groups", "band"), None, None), P(("groups", "band"), None, None)),
        check_vma=False,
    )
```

time: 103 us -> 88.8 us (0.86)
  the two profiles are of different devices: /device:TPU:21 before, /device:TPU:1 now
where the time goes in v2:
time: 88.8 us; the launch traced here: 88.6 us
  Pallas kernels  57.2 us (64%)
  starting transfers between devices  13.5 us (15%)
  local copies, waits for them, and re-layouts  8.35 us (9%)
  waiting for transfers between devices  6.8 us (8%)
  other arithmetic  1.91 us (2%)
    pallas_call x1, Pallas kernels, attention(): pl.pallas_call(main_kernel, grid=grid, out_shape=jax.ShapeDtypeStruct(que...  30.5 us
    pallas_call x1, Pallas kernels, attention(): pl.pallas_call(functools.partial(edge_kernel, col_shift.shape[0], rows),...  13.5 us
    pallas_call x1, Pallas kernels, decoder(): pl.pallas_call(functools.partial(decoder_kernel, group), out_shape=jax.Sh...  13.2 us
    ppermute x2, starting transfers between devices, to_next(): return lax.ppermute(block, axis, [(i, i + 1) for i in range(count - 1)])  9.5 us
    slice x7, local copies, waits for them, and re-layouts, decoder(): pixels[dy:dy + rows + 2]  5.33 us
    ppermute x2, waiting for transfers between devices, to_previous(): return lax.ppermute(block, axis, [(i + 1, i) for i in range(count - 1)])  4.25 us
    ppermute x2, starting transfers between devices, to_previous(): return lax.ppermute(block, axis, [(i + 1, i) for i in range(count - 1)])  4.02 us
    ppermute x2, waiting for transfers between devices, to_next(): return lax.ppermute(block, axis, [(i, i + 1) for i in range(count - 1)])  2.55 us
  transfers between devices with their start and end apart: 4, of which 2 were waited for; matrix products, arithmetic and copies ran while one was open for 9% of the time, Pallas kernels for 15%

profile of v2, /device:TPU:1, one launch (start us, length us, event | category | flops | bytes accessed | tf_op | source)
XLA Modules:
  0.0 88.6 jit_solution(12841685765545051505)
XLA Ops:
  0.6 0.0 copy-start.2
  0.6 1.2 %slice_bitcast_fusion = (bf16[80,2560]{1,0:T(8,128)(2,1)S(1)}, bf16[80,2560]{1,0:T(8,128)(2,1)S(1)}) fusion(bf16[4,80,2560]{2,1,0:T(8,128)(2,1)} %q_ref.1), kind=kLoop, calls=%fused_computation.4 | loop fusion | bytes 1638400 | tf_op jit(solution)/shard_map/squeeze | solution.py:324
  1.9 0.0 copy-done.2
  2.0 4.5 %collective-permute-start = (bf16[86,2560]{1,0:T(8,128)(2,1)S(1)}, bf16[86,2560]{1,0:T(8,128)(2,1)S(1)}, u32[]{:S(2)}, u32[]{:S(2)}) collective-permute-start(bf16[86,2560]{1,0:T(8,128)(2,1)S(1)} %pad_maximum_fusion.1), channel_id=1, source_target_pairs={{0,1},{1,2},{2,3},{3,4},{4,5},{5,6},{6,7},{7,8},{8,9},{9,10},{10,1... | collective-permute-start | bytes 1320968 | tf_op jit(solution)/shard_map/ppermute | solution.py:20
  6.6 1.9 %collective-permute-start.1 = (bf16[86,2560]{1,0:T(8,128)(2,1)S(1)}, bf16[86,2560]{1,0:T(8,128)(2,1)S(1)}, u32[]{:S(2)}, u32[]{:S(2)}) collective-permute-start(bf16[86,2560]{1,0:T(8,128)(2,1)S(1)} %pad_maximum_fusion.2), channel_id=1, source_target_pairs={{1,0},{2,1},{3,2},{4,3},{5,4},{6,5},{7,6},{8,7},{9,8},{10,9},{11,1... | collective-permute-start | bytes 1320968 | tf_op jit(solution)/shard_map/ppermute | solution.py:25
  8.5 0.8 concatenate.22
  9.3 2.6 %collective-permute-done.qp_ref = bf16[86,2560]{1,0:T(8,128)(2,1)S(1)} collective-permute-done((bf16[86,2560]{1,0:T(8,128)(2,1)S(1)}, bf16[86,2560]{1,0:T(8,128)(2,1)S(1)}, u32[]{:S(2)}, u32[]{:S(2)}) %collective-permute-start) | collective-permute-done | bytes 440352 | tf_op jit(solution)/shard_map/ppermute | solution.py:20
  11.8 0.0 copy-start
  11.8 0.2 concatenate.21
  12.0 4.2 %collective-permute-done.1.qn_ref = bf16[86,2560]{1,0:T(8,128)(2,1)S(1)} collective-permute-done((bf16[86,2560]{1,0:T(8,128)(2,1)S(1)}, bf16[86,2560]{1,0:T(8,128)(2,1)S(1)}, u32[]{:S(2)}, u32[]{:S(2)}) %collective-permute-start.1) | collective-permute-done | bytes 440352 | tf_op jit(solution)/shard_map/ppermute | solution.py:25
  16.3 0.0 copy-start.1
  16.3 0.2 concatenate.23
  16.5 0.0 copy-done
  16.5 0.5 copy-done.1
  17.1 13.5 %edge_attention.1 = (bf16[80,2944]{1,0:T(8,128)(2,1)}, bf16[80,2944]{1,0:T(8,128)(2,1)}) custom-call(s32[64]{0:T(128)} %shift_ref.3, s32[3]{0:T(128)} %mask_ref.3, bf16[86,2560]{1,0:T(8,128)(2,1)} %copy-done, bf16[86,2560]{1,0:T(8,128)(2,1)} %copy-done.1, bf16[2,4,4,80,2560]{4,3,2,1,0:T(8,128)(2,1)} %kv_ref.1, bf16[2,4,4,80,2560]{4,3,2,1,0:T(8,128)(2,1)} %kv_ref.1), custom_call_target="tpu_custom_call" | custom-call | flops 524288000 | bytes 6553600 | tf_op jit(solution)/shard_map/edge_attention/pallas_call | solution.py:190
  30.5 5.0 %collective-permute-start.2 = (bf16[80,2944]{1,0:T(8,128)(2,1)}, bf16[80,2944]{1,0:T(8,128)(2,1)}, u32[]{:S(2)}, u32[]{:S(2)}) collective-permute-start(bf16[80,2944]{1,0:T(8,128)(2,1)} %get-tuple-element.4), channel_id=1, source_target_pairs={{0,1},{1,2},{2,3},{3,4},{4,5},{5,6},{6,7},{7,8},{8,9},{9,10},{10,1... | collective-permute-start | bytes 1413128 | tf_op jit(solution)/shard_map/ppermute | solution.py:20
  35.5 2.1 %collective-permute-start.3 = (bf16[80,2944]{1,0:T(8,128)(2,1)}, bf16[80,2944]{1,0:T(8,128)(2,1)}, u32[]{:S(2)}, u32[]{:S(2)}) collective-permute-start(bf16[80,2944]{1,0:T(8,128)(2,1)} %get-tuple-element.5), channel_id=1, source_target_pairs={{1,0},{2,1},{3,2},{4,3},{5,4},{6,5},{7,6},{8,7},{9,8},{10,9},{11,1... | collective-permute-start | bytes 1413128 | tf_op jit(solution)/shard_map/ppermute | solution.py:25
  37.6 0.3 maximum_bitcast_fusion
  38.0 1.6 %fusion = (bf16[10,160,3,16]{3,1,0,2:T(8,128)(2,1)}, bf16[10,160,3,16]{3,1,0,2:T(8,128)(2,1)S(1)}, bf16[10,160,3,16]{3,1,0,2:T(8,128)(2,1)S(1)}) fusion(bf16[12,160,3,16]{3,1,0,2:T(8,128)(2,1)S(1)} %maximum_bitcast_fusion), kind=kLoop, calls=%fused_computation.6 | loop fusion | bytes 921600 | tf_op jit(solution)/shard_map/slice | solution.py:296
  39.6 1.8 %copy.28 = bf16[10,160,3,16]{1,3,2,0:T(8,128)(2,1)S(1)} copy(bf16[10,160,3,16]{3,1,0,2:T(8,128)(2,1)} %get-tuple-element.8) | data formatting | bytes 307200 | tf_op jit(solution)/shard_map/slice | solution.py:296
  41.4 0.3 copy.31
  41.7 0.6 copy.29
  42.2 0.3 copy.32
  42.5 0.6 copy.30
  43.0 0.3 copy.33
  43.3 1.5 %pad_maximum_fusion.lat_ref = bf16[10,160,144]{2,1,0:T(8,128)(2,1)} fusion(bf16[10,160,48]{2,1,0:T(8,128)(2,1)S(1)} %copy.33, bf16[10,160,48]{2,1,0:T(8,128)(2,1)S(1)} %copy.32, bf16[10,160,48]{2,1,0:T(8,128)(2,1)S(1)} %copy.31), kind=kLoop, calls=%fused_computation.1 | loop fusion | flops 1382400 | bytes 921600 | tf_op jit(solution)/shard_map/concatenate | solution.py:296
  44.8 13.2 %decoder.1 = bf16[8,160,384]{2,1,0:T(8,128)(2,1)} custom-call(bf16[10,160,144]{2,1,0:T(8,128)(2,1)} %pad_maximum_fusion.lat_ref, bf16[432,384]{1,0:T(8,128)(2,1)} %cin_ref.1, bf16[3456,384]{1,0:T(8,128)(2,1)} %wmid_ref.1, f32[384]{0:T(512)} %bin_ref.1, f32[384]{0:T(512)} %gain_ref.1, f32[384]{0:T(512)} %bmid_ref.1), custom_call_target="tpu_custom_call" | custom-call | flops 3397386240 | bytes 2654208 | tf_op jit(solution)/shard_map/decoder/pallas_call | solution.py:299
  58.0 0.0 collective-permute-done.2.op_ref
  58.0 0.0 collective-permute-done.3.on_ref
  58.0 30.5 %main_attention.1 = bf16[4,80,2560]{2,1,0:T(8,128)(2,1)} custom-call(s32[64]{0:T(128)} %shift_ref.3, s32[3]{0:T(128)} %mask_ref.3, bf16[4,80,2560]{2,1,0:T(8,128)(2,1)} %q_ref.1, bf16[2,4,4,80,2560]{4,3,2,1,0:T(8,128)(2,1)} %kv_ref.1, bf16[80,2944]{1,0:T(8,128)(2,1)} %collective-permute-done.2.op_ref, bf16[80,2944]{1,0:T(8,128)(2,1)} %collective-permute-done.3.on_ref), custom_call_target="tpu_custom_call" | custom-call | flops 3145728000 | bytes 13107200 | tf_op jit(solution)/shard_map/main_attention/pallas_call | solution.py:213
  (7 shorter events, 0.2 us)
Async XLA Ops:
  0.6 1.2 %copy-start.2 = (bf16[3,8,2560]{2,1,0:T(8,128)(2,1)S(1)}, bf16[3,8,2560]{2,1,0:T(8,128)(2,1)}, u32[]{:S(2)}) copy-start(bf16[3,8,2560]{2,1,0:T(8,128)(2,1)} %param.14) | copy-start | bytes 368644
  2.0 9.8 %collective-permute-start = (bf16[86,2560]{1,0:T(8,128)(2,1)S(1)}, bf16[86,2560]{1,0:T(8,128)(2,1)S(1)}, u32[]{:S(2)}, u32[]{:S(2)}) collective-permute-start(bf16[86,2560]{1,0:T(8,128)(2,1)S(1)} %pad_maximum_fusion.1), channel_id=1, source_target_pairs={{0,1},{1,2},{2,3},{3,4},{4,5},{5,6},{6,7},{7,8},{8,9},{9,10},{10,1... | collective-permute-start | bytes 1320968 | tf_op jit(solution)/shard_map/ppermute | solution.py:20
  6.6 9.7 %collective-permute-start.1 = (bf16[86,2560]{1,0:T(8,128)(2,1)S(1)}, bf16[86,2560]{1,0:T(8,128)(2,1)S(1)}, u32[]{:S(2)}, u32[]{:S(2)}) collective-permute-start(bf16[86,2560]{1,0:T(8,128)(2,1)S(1)} %pad_maximum_fusion.2), channel_id=1, source_target_pairs={{1,0},{2,1},{3,2},{4,3},{5,4},{6,5},{7,6},{8,7},{9,8},{10,9},{11,1... | collective-permute-start | bytes 1320968 | tf_op jit(solution)/shard_map/ppermute | solution.py:25
  11.8 4.7 %copy-start = (bf16[86,2560]{1,0:T(8,128)(2,1)}, bf16[86,2560]{1,0:T(8,128)(2,1)S(1)}, u32[]{:S(2)}) copy-start(bf16[86,2560]{1,0:T(8,128)(2,1)S(1)} %collective-permute-done.qp_ref) | copy-start | bytes 1320964
  16.3 0.8 copy-start.1
  30.5 27.5 %collective-permute-start.2 = (bf16[80,2944]{1,0:T(8,128)(2,1)}, bf16[80,2944]{1,0:T(8,128)(2,1)}, u32[]{:S(2)}, u32[]{:S(2)}) collective-permute-start(bf16[80,2944]{1,0:T(8,128)(2,1)} %get-tuple-element.4), channel_id=1, source_target_pairs={{0,1},{1,2},{2,3},{3,4},{4,5},{5,6},{6,7},{7,8},{8,9},{9,10},{10,1... | collective-permute-start | bytes 1413128 | tf_op jit(solution)/shard_map/ppermute | solution.py:20
  35.5 22.5 %collective-permute-start.3 = (bf16[80,2944]{1,0:T(8,128)(2,1)}, bf16[80,2944]{1,0:T(8,128)(2,1)}, u32[]{:S(2)}, u32[]{:S(2)}) collective-permute-start(bf16[80,2944]{1,0:T(8,128)(2,1)} %get-tuple-element.5), channel_id=1, source_target_pairs={{1,0},{2,1},{3,2},{4,3},{5,4},{6,5},{7,6},{8,7},{9,8},{10,9},{11,1... | collective-permute-start | bytes 1413128 | tf_op jit(solution)/shard_map/ppermute | solution.py:25
